TPU v7x, 768 devices: a whole 4x8x12 slice. The times are simulated.
768 devices in a mesh: blk: 192 (over z_hi, x, y, core), fsdp: 4 (over z_lo).
Axes of the slice: x: 4, y: 8, z: 12 (z_hi: 3, z_lo: 4; z = z_hi * 4 + z_lo), core: 2. Of those that a mesh axis runs over, the one named last changes fastest.
Arguments:
- hidden_in: bfloat16 [4, 98304, 2048], P('fsdp', 'blk'), may hold values from -6 to 6
- w_query: bfloat16 [2048, 128], P('fsdp'), may hold values from -0.125 to 0.125
- query_gain: float32 [128], replicated, may hold values from 0.1 to 1.9
- key_rows: bfloat16 [4, 98304, 128], P('fsdp', 'blk'), may hold values from -4 to 4
- value_rows: bfloat16 [4, 98304, 128], P('fsdp', 'blk'), may hold values from -6 to 6
- grad_out: bfloat16 [4, 98304, 128], P('fsdp', 'blk'), may hold values from -6 to 6
- logsumexp: float32 [4, 98304], P('fsdp', 'blk'), may hold values from 4 to 8
- row_delta: float32 [4, 98304], P('fsdp', 'blk'), may hold values from -6 to 6
- doc_ids: int32 [4, 98304], P('fsdp', 'blk'), may hold values from 0 to 95, never falling along the last dimension, each value on 1 to 4096 neighbouring positions
Outputs:
- grad_hidden: bfloat16 [4, 98304, 2048], P('fsdp', 'blk')
- grad_keys: bfloat16 [4, 98304, 128], P('fsdp', 'blk')
- grad_values: bfloat16 [4, 98304, 128], P('fsdp', 'blk')
- grad_wquery: float32 [2048, 128], P('fsdp')
Inputs may be any that keep to these rules, and one draw needn't show every extreme that they name: `doc_ids`: along each sequence the document numbers never fall; each document has 1 to 4096 tokens.
All inputs are finite; a program needn't handle non-finite values.
Results may differ from a plain program's by a relative error of at most 0.0097.
Values may be sent and summed in bfloat16 or wider, within the bound.
A program may use at most 64 MiB of HBM per device.

v0:
```python
import jax
import jax.numpy as jnp
from jax import lax
from jax.sharding import PartitionSpec as P

ROUNDS = 8


def sent_to_all(value, axis):
    copies = jnp.broadcast_to(value, (lax.axis_size(axis), *value.shape))
    return lax.all_to_all(copies, axis, split_axis=0, concat_axis=0, tiled=True)


def in_order(tiles, dim):
    dims = list(tiles.shape[1:])
    dims[dim] *= tiles.shape[0]
    return jnp.moveaxis(tiles, 0, dim).reshape(dims)


def collect(value, axis, dim):
    tiles = sent_to_all(value, axis)
    return in_order(tiles, dim)


def passed_along(value, axis, by):
    size = lax.axis_size(axis)
    pairs = [(i, i + by) for i in range(size) if 0 <= i + by < size]
    return lax.ppermute(value, axis, pairs)


def from_behind(value, axis, by):
    size = lax.axis_size(axis)
    return lax.ppermute(value, axis, [(i, (i + by) % size) for i in range(size)])


def local(
    hidden_in, w_query, query_gain, key_rows, value_rows, grad_out, logsumexp, row_delta, doc_ids
):
    inputs = hidden_in[0]
    own_keys = key_rows[0]
    own_values = value_rows[0]
    outgrad = grad_out[0]
    own_lse = logsumexp[0]
    own_delta = row_delta[0]
    own_docs = doc_ids[0].astype(jnp.float32)
    tokens = own_keys.shape[0]
    width = own_keys.shape[1]
    score_scale = width ** (-0.5)
    position = lax.axis_index("blk")
    cycle_size = lax.axis_size("blk")
    lower_tri = jnp.arange(tokens)[:, None] >= jnp.arange(tokens)[None, :]
    projection = collect(w_query, "fsdp", 0)
    q_pre = jnp.dot(inputs, projection, preferred_element_type=jnp.float32)
    inverse = lax.rsqrt(jnp.mean(q_pre * q_pre, axis=-1, keepdims=True) + 1e-06)
    normed = q_pre * inverse
    query = (normed * query_gain).astype(jnp.bfloat16)
    zeros_rows = jnp.zeros((tokens, width), jnp.float32)
    row_pair = jnp.stack([query, outgrad])
    lse_far, delta_far, docs_far, query_acc = (own_lse, own_delta, own_docs, zeros_rows)
    keys_acc, values_acc = (zeros_rows, zeros_rows)
    for turn in range(ROUNDS):
        if turn > 0:
            row_pair = passed_along(row_pair, "blk", -1)
            lse_far, delta_far, docs_far, query_acc = from_behind(
                (lse_far, delta_far, docs_far, query_acc), "blk", -1
            )
        in_range = position + turn < cycle_size
        q_block = row_pair[0]
        o_block = row_pair[1]
        allowed = (docs_far[:, None] == own_docs[None, :]) & in_range
        if turn == 0:
            allowed = allowed & lower_tri
        scores = (
            lax.dot_general(
                q_block, own_keys, (((1,), (1,)), ((), ())), preferred_element_type=jnp.float32
            )
            * score_scale
        )
        attn_prob = jnp.exp(jnp.where(allowed, scores - lse_far[:, None], -1e30))
        grad_prob = lax.dot_general(
            o_block, own_values, (((1,), (1,)), ((), ())), preferred_element_type=jnp.float32
        )
        grad_score = attn_prob * (grad_prob - delta_far[:, None])
        prob_half = attn_prob.astype(jnp.bfloat16)
        score_half = grad_score.astype(jnp.bfloat16)
        query_term = jnp.dot(score_half, own_keys, preferred_element_type=jnp.float32)
        key_term = lax.dot_general(
            score_half, q_block, (((0,), (0,)), ((), ())), preferred_element_type=jnp.float32
        )
        value_term = lax.dot_general(
            prob_half, o_block, (((0,), (0,)), ((), ())), preferred_element_type=jnp.float32
        )
        query_term, key_term, value_term = (query_term, key_term, value_term)
        query_acc = query_acc + query_term
        keys_acc = keys_acc + key_term
        values_acc = values_acc + value_term
    grad_query = from_behind(query_acc, "blk", ROUNDS - 1) * score_scale
    grad_keys = (keys_acc * score_scale).astype(jnp.bfloat16)
    grad_values = values_acc.astype(jnp.bfloat16)
    scaled = grad_query * query_gain
    grad_pre = (
        inverse * (scaled - normed * jnp.mean(scaled * normed, axis=-1, keepdims=True))
    ).astype(jnp.bfloat16)
    grad_hidden = lax.dot_general(
        grad_pre, projection, (((1,), (1,)), ((), ())), preferred_element_type=jnp.float32
    )
    weight_term = lax.dot_general(
        inputs, grad_pre, (((0,), (0,)), ((), ())), preferred_element_type=jnp.float32
    )
    weight_sum = lax.psum(weight_term, ("blk", "fsdp"))
    owned = w_query.shape[0]
    grad_wquery = lax.dynamic_slice_in_dim(weight_sum, lax.axis_index("fsdp") * owned, owned, 0)
    return (grad_hidden.astype(jnp.bfloat16)[None], grad_keys[None], grad_values[None], grad_wquery)


def solution(mesh):
    return jax.shard_map(
        local,
        mesh=mesh,
        in_specs=(
            P("fsdp", "blk", None),
            P("fsdp", None),
            P(),
            P("fsdp", "blk", None),
            P("fsdp", "blk", None),
            P("fsdp", "blk", None),
            P("fsdp", "blk"),
            P("fsdp", "blk"),
            P("fsdp", "blk"),
        ),
        out_specs=(
            P("fsdp", "blk", None),
            P("fsdp", "blk", None),
            P("fsdp", "blk", None),
            P("fsdp", None),
        ),
        check_vma=False,
    )
```

profile of v0, /device:TPU:1, one launch (start us, length us, event | category | flops | bytes accessed | tf_op | source)
XLA Modules:
  0.0 817.5 jit_solution(10110281511561840347)
XLA Ops:
  7.2 1.9 broadcast_in_dim.19
  9.1 7.9 all-to-all-start
  17.1 8.1 collective-permute-start.3
  25.2 0.7 convert_element_type.74
  25.9 11.0 %collective-permute-start.1 = (f32[512]{0:T(512)S(1)}, f32[512]{0:T(512)S(1)}, u32[]{:S(2)}, u32[]{:S(2)}) collective-permute-start(f32[512]{0:T(512)S(1)} %bitcast.156), channel_id=1, source_target_pairs={{0,764},{4,0},{8,4},{12,8},{16,12},{20,16},{24,20},{28,24},{32,28}... | collective-permute-start | bytes 6152 | tf_op jit(solution)/shard_map/ppermute | solution.py:33
  36.9 2.9 collective-permute-start.4
  39.8 2.4 collective-permute-start.8
  42.2 7.3 collective-permute-start.6
  49.6 3.2 collective-permute-start.9
  52.8 2.6 collective-permute-start.13
  55.4 7.1 collective-permute-start.11
  62.6 3.2 collective-permute-start.14
  65.8 2.6 collective-permute-start.18
  68.4 7.1 collective-permute-start.16
  75.6 3.2 collective-permute-start.19
  78.8 2.6 collective-permute-start.23
  81.5 7.1 collective-permute-start.21
  88.6 3.2 collective-permute-start.24
  91.8 0.7 broadcast_multiply_fusion.1
  92.5 2.6 collective-permute-start.28
  95.1 6.5 collective-permute-start.26
  101.6 3.2 collective-permute-start.29
  104.9 1.0 copy.14
  105.9 2.6 collective-permute-start.33
  108.6 6.1 collective-permute-start.31
  114.7 3.3 collective-permute-start.34
  118.0 0.8 multiply_reduce_fusion.1
  119.0 2.6 collective-permute-start.2
  121.7 0.5 fusion.6
  123.3 1.9 collective-permute-start
  125.5 1.2 collective-permute-done.2
  127.6 3.4 collective-permute-done
  131.3 5.2 collective-permute-start.5
  136.5 12.1 %collective-permute-start.7 = (bf16[2,512,128]{1,2,0:T(8,128)(2,1)S(1)}, bf16[2,512,128]{1,2,0:T(8,128)(2,1)S(1)}, u32[]{:S(2)}, u32[]{:S(2)}) collective-permute-start(bf16[2,512,128]{1,2,0:T(8,128)(2,1)S(1)} %collective-permute-done.2), channel_id=1, source_target_pairs={{4,0},{8,4},{12,8},{16,12},{20,16},{24,20},{28,24},{32,28},{36,32}... | collective-permute-start | bytes 786440 | tf_op jit(solution)/shard_map/ppermute | solution.py:28
  149.0 0.5 convolution_add_fusion.6
  151.0 2.3 collective-permute-start.10
  153.2 11.3 %collective-permute-start.12 = (bf16[2,512,128]{1,2,0:T(8,128)(2,1)S(1)}, bf16[2,512,128]{1,2,0:T(8,128)(2,1)S(1)}, u32[]{:S(2)}, u32[]{:S(2)}) collective-permute-start(bf16[2,512,128]{1,2,0:T(8,128)(2,1)S(1)} %collective-permute-done.7), channel_id=1, source_target_pairs={{4,0},{8,4},{12,8},{16,12},{20,16},{24,20},{28,24},{32,28},{36,32}... | collective-permute-start | bytes 786440 | tf_op jit(solution)/shard_map/ppermute | solution.py:28
  164.9 0.5 convolution_add_fusion.5
  166.9 2.3 collective-permute-start.15
  169.2 11.2 %collective-permute-start.17 = (bf16[2,512,128]{1,2,0:T(8,128)(2,1)S(1)}, bf16[2,512,128]{1,2,0:T(8,128)(2,1)S(1)}, u32[]{:S(2)}, u32[]{:S(2)}) collective-permute-start(bf16[2,512,128]{1,2,0:T(8,128)(2,1)S(1)} %collective-permute-done.12), channel_id=1, source_target_pairs={{4,0},{8,4},{12,8},{16,12},{20,16},{24,20},{28,24},{32,28},{36,32}... | collective-permute-start | bytes 786440 | tf_op jit(solution)/shard_map/ppermute | solution.py:28
  180.8 0.5 convolution_add_fusion.4
  182.8 2.3 collective-permute-start.20
  185.1 11.5 %collective-permute-start.22 = (bf16[2,512,128]{1,2,0:T(8,128)(2,1)S(1)}, bf16[2,512,128]{1,2,0:T(8,128)(2,1)S(1)}, u32[]{:S(2)}, u32[]{:S(2)}) collective-permute-start(bf16[2,512,128]{1,2,0:T(8,128)(2,1)S(1)} %collective-permute-done.17), channel_id=1, source_target_pairs={{4,0},{8,4},{12,8},{16,12},{20,16},{24,20},{28,24},{32,28},{36,32}... | collective-permute-start | bytes 786440 | tf_op jit(solution)/shard_map/ppermute | solution.py:28
  196.9 0.6 convolution_add_fusion.3
  198.7 2.3 collective-permute-start.25
  201.0 11.3 %collective-permute-start.27 = (bf16[2,512,128]{1,2,0:T(8,128)(2,1)S(1)}, bf16[2,512,128]{1,2,0:T(8,128)(2,1)S(1)}, u32[]{:S(2)}, u32[]{:S(2)}) collective-permute-start(bf16[2,512,128]{1,2,0:T(8,128)(2,1)S(1)} %collective-permute-done.22), channel_id=1, source_target_pairs={{4,0},{8,4},{12,8},{16,12},{20,16},{24,20},{28,24},{32,28},{36,32}... | collective-permute-start | bytes 786440 | tf_op jit(solution)/shard_map/ppermute | solution.py:28
  212.7 0.5 convolution_add_fusion.2
  213.8 2.3 collective-permute-start.32
  216.1 1.2 fusion.23
  217.7 1.9 collective-permute-start.30
  219.6 2.7 collective-permute-done.32
  223.0 1.2 fusion.22
  224.5 0.9 collective-permute-done.30
  225.4 1.9 collective-permute-start.35
  227.3 1.9 convolution_add_fusion.1
  229.2 15.5 %collective-permute-done.35 = f32[512,128]{0,1:T(8,128)S(1)} collective-permute-done((f32[512,128]{0,1:T(8,128)S(1)}, f32[512,128]{0,1:T(8,128)S(1)}, u32[]{:S(2)}, u32[]{:S(2)}) %collective-permute-start.35) | collective-permute-done | bytes 262176 | tf_op jit(solution)/shard_map/ppermute | solution.py:33
  245.0 1.4 convolution_bitcast_fusion
  246.5 1.4 convolution_add_fusion.8
  247.9 2.1 fusion.34
  250.0 1.9 fusion.33
  251.8 2.1 fusion
  253.9 554.9 %all-reduce.2.cloned.1.call-done = f32[2048,128]{0,1:T(8,128)} async-done(((f32[2048,128]{0,1:T(8,128)}), f32[2048,128]{0,1:T(8,128)}) %all-reduce.2.cloned.1.call-update) | async-done | bytes 1048592 | tf_op jit(solution)/shard_map/psum | solution.py:110
  808.8 1.0 constant_dynamic-slice_fusion
  809.8 0.8 copy.22
  (102 shorter events, 12.1 us)
Async XLA Ops:
  7.2 110.8 %copy-start = (bf16[1,512,2048]{2,1,0:T(8,128)(2,1)S(1)}, bf16[1,512,2048]{2,1,0:T(8,128)(2,1)}, u32[]{:S(2)}) copy-start(bf16[1,512,2048]{2,1,0:T(8,128)(2,1)} %param.9) | copy-start | bytes 6291460
  9.1 109.8 %copy-start.10 = (f32[128]{0:T(128)S(1)}, f32[128]{0:T(128)}, u32[]{:S(2)}) copy-start(f32[128]{0:T(128)} %param.11) | copy-start | bytes 1540
  9.1 108.9 %all-to-all-start = ((bf16[4,512,128]{2,1,0:T(8,128)(2,1)}), bf16[4,512,128]{2,1,0:T(8,128)(2,1)S(1)}, u32[]{:S(2)}, u32[]{:S(2)}) async-start(bf16[4,512,128]{2,1,0:T(8,128)(2,1)} %broadcast_in_dim.19), calls=%async_computation | async-start | bytes 1048576 | tf_op jit(solution)/shard_map/all_to_all | solution.py:11
  17.0 104.6 %copy-start.1 = (bf16[1,512,128]{2,1,0:T(8,128)(2,1)S(1)}, bf16[1,512,128]{2,1,0:T(8,128)(2,1)}, u32[]{:S(2)}) copy-start(bf16[1,512,128]{2,1,0:T(8,128)(2,1)} %param.12) | copy-start | bytes 393220
  17.0 104.6 %copy-start.12 = (f32[1,512]{1,0:T(1,128)S(1)}, f32[1,512]{1,0:T(1,128)}, u32[]{:S(2)}) copy-start(f32[1,512]{1,0:T(1,128)} %param.15) | copy-start | bytes 6148
  17.0 791.8 %all-reduce.2.cloned.1.call-start = ((), (), s32[]{:S(2)}) async-start(), calls=%async_computation.1 | async-start | bytes 2097152 | tf_op jit(solution)/shard_map/psum | solution.py:110
  17.1 22.7 %collective-permute-start.3 = (f32[512]{0:T(512)}, f32[512]{0:T(512)S(1)}, u32[]{:S(2)}, u32[]{:S(2)}) collective-permute-start(f32[512]{0:T(512)} %bitcast.174), channel_id=1, source_target_pairs={{0,764},{4,0},{8,4},{12,8},{16,12},{20,16},{24,20},{28,24},{32,28}... | collective-permute-start | bytes 6152 | tf_op jit(solution)/shard_map/ppermute | solution.py:33
  25.9 16.3 %collective-permute-start.1 = (f32[512]{0:T(512)S(1)}, f32[512]{0:T(512)S(1)}, u32[]{:S(2)}, u32[]{:S(2)}) collective-permute-start(f32[512]{0:T(512)S(1)} %bitcast.156), channel_id=1, source_target_pairs={{0,764},{4,0},{8,4},{12,8},{16,12},{20,16},{24,20},{28,24},{32,28}... | collective-permute-start | bytes 6152 | tf_op jit(solution)/shard_map/ppermute | solution.py:33
  36.9 12.7 %collective-permute-start.4 = (f32[512]{0:T(512)}, f32[512]{0:T(512)S(1)}, u32[]{:S(2)}, u32[]{:S(2)}) collective-permute-start(f32[512]{0:T(512)} %bitcast.172), channel_id=1, source_target_pairs={{0,764},{4,0},{8,4},{12,8},{16,12},{20,16},{24,20},{28,24},{32,28}... | collective-permute-start | bytes 6152 | tf_op jit(solution)/shard_map/ppermute | solution.py:33
  39.8 13.0 %collective-permute-start.8 = (f32[512]{0:T(512)S(1)}, f32[512]{0:T(512)S(1)}, u32[]{:S(2)}, u32[]{:S(2)}) collective-permute-start(f32[512]{0:T(512)S(1)} %collective-permute-done.3), channel_id=1, source_target_pairs={{0,764},{4,0},{8,4},{12,8},{16,12},{20,16},{24,20},{28,24},{32,28}... | collective-permute-start | bytes 6152 | tf_op jit(solution)/shard_map/ppermute | solution.py:33
  42.2 13.2 %collective-permute-start.6 = (f32[512]{0:T(512)S(1)}, f32[512]{0:T(512)S(1)}, u32[]{:S(2)}, u32[]{:S(2)}) collective-permute-start(f32[512]{0:T(512)S(1)} %collective-permute-done.1), channel_id=1, source_target_pairs={{0,764},{4,0},{8,4},{12,8},{16,12},{20,16},{24,20},{28,24},{32,28}... | collective-permute-start | bytes 6152 | tf_op jit(solution)/shard_map/ppermute | solution.py:33
  49.6 13.0 %collective-permute-start.9 = (f32[512]{0:T(512)S(1)}, f32[512]{0:T(512)S(1)}, u32[]{:S(2)}, u32[]{:S(2)}) collective-permute-start(f32[512]{0:T(512)S(1)} %collective-permute-done.4), channel_id=1, source_target_pairs={{0,764},{4,0},{8,4},{12,8},{16,12},{20,16},{24,20},{28,24},{32,28}... | collective-permute-start | bytes 6152 | tf_op jit(solution)/shard_map/ppermute | solution.py:33
  52.8 13.0 %collective-permute-start.13 = (f32[512]{0:T(512)S(1)}, f32[512]{0:T(512)S(1)}, u32[]{:S(2)}, u32[]{:S(2)}) collective-permute-start(f32[512]{0:T(512)S(1)} %collective-permute-done.8), channel_id=1, source_target_pairs={{0,764},{4,0},{8,4},{12,8},{16,12},{20,16},{24,20},{28,24},{32,28}... | collective-permute-start | bytes 6152 | tf_op jit(solution)/shard_map/ppermute | solution.py:33
  55.4 13.0 %collective-permute-start.11 = (f32[512]{0:T(512)S(1)}, f32[512]{0:T(512)S(1)}, u32[]{:S(2)}, u32[]{:S(2)}) collective-permute-start(f32[512]{0:T(512)S(1)} %collective-permute-done.6), channel_id=1, source_target_pairs={{0,764},{4,0},{8,4},{12,8},{16,12},{20,16},{24,20},{28,24},{32,28}... | collective-permute-start | bytes 6152 | tf_op jit(solution)/shard_map/ppermute | solution.py:33
  62.6 13.0 %collective-permute-start.14 = (f32[512]{0:T(512)S(1)}, f32[512]{0:T(512)S(1)}, u32[]{:S(2)}, u32[]{:S(2)}) collective-permute-start(f32[512]{0:T(512)S(1)} %collective-permute-done.9), channel_id=1, source_target_pairs={{0,764},{4,0},{8,4},{12,8},{16,12},{20,16},{24,20},{28,24},{32,28}... | collective-permute-start | bytes 6152 | tf_op jit(solution)/shard_map/ppermute | solution.py:33
  65.8 13.0 %collective-permute-start.18 = (f32[512]{0:T(512)S(1)}, f32[512]{0:T(512)S(1)}, u32[]{:S(2)}, u32[]{:S(2)}) collective-permute-start(f32[512]{0:T(512)S(1)} %collective-permute-done.13), channel_id=1, source_target_pairs={{0,764},{4,0},{8,4},{12,8},{16,12},{20,16},{24,20},{28,24},{32,28}... | collective-permute-start | bytes 6152 | tf_op jit(solution)/shard_map/ppermute | solution.py:33
  68.4 13.0 %collective-permute-start.16 = (f32[512]{0:T(512)S(1)}, f32[512]{0:T(512)S(1)}, u32[]{:S(2)}, u32[]{:S(2)}) collective-permute-start(f32[512]{0:T(512)S(1)} %collective-permute-done.11), channel_id=1, source_target_pairs={{0,764},{4,0},{8,4},{12,8},{16,12},{20,16},{24,20},{28,24},{32,28}... | collective-permute-start | bytes 6152 | tf_op jit(solution)/shard_map/ppermute | solution.py:33
  75.6 13.0 %collective-permute-start.19 = (f32[512]{0:T(512)S(1)}, f32[512]{0:T(512)S(1)}, u32[]{:S(2)}, u32[]{:S(2)}) collective-permute-start(f32[512]{0:T(512)S(1)} %collective-permute-done.14), channel_id=1, source_target_pairs={{0,764},{4,0},{8,4},{12,8},{16,12},{20,16},{24,20},{28,24},{32,28}... | collective-permute-start | bytes 6152 | tf_op jit(solution)/shard_map/ppermute | solution.py:33
  78.8 13.7 %collective-permute-start.23 = (f32[512]{0:T(512)S(1)}, f32[512]{0:T(512)S(1)}, u32[]{:S(2)}, u32[]{:S(2)}) collective-permute-start(f32[512]{0:T(512)S(1)} %collective-permute-done.18), channel_id=1, source_target_pairs={{0,764},{4,0},{8,4},{12,8},{16,12},{20,16},{24,20},{28,24},{32,28}... | collective-permute-start | bytes 6152 | tf_op jit(solution)/shard_map/ppermute | solution.py:33
  81.5 13.7 %collective-permute-start.21 = (f32[512]{0:T(512)S(1)}, f32[512]{0:T(512)S(1)}, u32[]{:S(2)}, u32[]{:S(2)}) collective-permute-start(f32[512]{0:T(512)S(1)} %collective-permute-done.16), channel_id=1, source_target_pairs={{0,764},{4,0},{8,4},{12,8},{16,12},{20,16},{24,20},{28,24},{32,28}... | collective-permute-start | bytes 6152 | tf_op jit(solution)/shard_map/ppermute | solution.py:33
  88.6 13.0 %collective-permute-start.24 = (f32[512]{0:T(512)S(1)}, f32[512]{0:T(512)S(1)}, u32[]{:S(2)}, u32[]{:S(2)}) collective-permute-start(f32[512]{0:T(512)S(1)} %collective-permute-done.19), channel_id=1, source_target_pairs={{0,764},{4,0},{8,4},{12,8},{16,12},{20,16},{24,20},{28,24},{32,28}... | collective-permute-start | bytes 6152 | tf_op jit(solution)/shard_map/ppermute | solution.py:33
  92.5 13.4 %collective-permute-start.28 = (f32[512]{0:T(512)S(1)}, f32[512]{0:T(512)S(1)}, u32[]{:S(2)}, u32[]{:S(2)}) collective-permute-start(f32[512]{0:T(512)S(1)} %collective-permute-done.23), channel_id=1, source_target_pairs={{0,764},{4,0},{8,4},{12,8},{16,12},{20,16},{24,20},{28,24},{32,28}... | collective-permute-start | bytes 6152 | tf_op jit(solution)/shard_map/ppermute | solution.py:33
  95.1 13.4 %collective-permute-start.26 = (f32[512]{0:T(512)S(1)}, f32[512]{0:T(512)}, u32[]{:S(2)}, u32[]{:S(2)}) collective-permute-start(f32[512]{0:T(512)S(1)} %collective-permute-done.21), channel_id=1, source_target_pairs={{0,764},{4,0},{8,4},{12,8},{16,12},{20,16},{24,20},{28,24},{32,28}... | collective-permute-start | bytes 6152 | tf_op jit(solution)/shard_map/ppermute | solution.py:33
  101.6 13.0 %collective-permute-start.29 = (f32[512]{0:T(512)S(1)}, f32[512]{0:T(512)}, u32[]{:S(2)}, u32[]{:S(2)}) collective-permute-start(f32[512]{0:T(512)S(1)} %collective-permute-done.24), channel_id=1, source_target_pairs={{0,764},{4,0},{8,4},{12,8},{16,12},{20,16},{24,20},{28,24},{32,28}... | collective-permute-start | bytes 6152 | tf_op jit(solution)/shard_map/ppermute | solution.py:33
  105.9 113.7 %collective-permute-start.33 = (f32[512]{0:T(512)S(1)}, f32[512]{0:T(512)S(1)}, u32[]{:S(2)}, u32[]{:S(2)}) collective-permute-start(f32[512]{0:T(512)S(1)} %collective-permute-done.28), channel_id=1, source_target_pairs={{0,764},{4,0},{8,4},{12,8},{16,12},{20,16},{24,20},{28,24},{32,28}... | collective-permute-start | bytes 6152 | tf_op jit(solution)/shard_map/ppermute | solution.py:33
  108.6 114.1 %collective-permute-start.31 = (f32[512]{0:T(512)}, f32[512]{0:T(512)}, u32[]{:S(2)}, u32[]{:S(2)}) collective-permute-start(f32[512]{0:T(512)} %collective-permute-done.26), channel_id=1, source_target_pairs={{0,764},{4,0},{8,4},{12,8},{16,12},{20,16},{24,20},{28,24},{32,28}... | collective-permute-start | bytes 6152 | tf_op jit(solution)/shard_map/ppermute | solution.py:33
  114.7 108.0 %collective-permute-start.34 = (f32[512]{0:T(512)}, f32[512]{0:T(512)}, u32[]{:S(2)}, u32[]{:S(2)}) collective-permute-start(f32[512]{0:T(512)} %collective-permute-done.29), channel_id=1, source_target_pairs={{0,764},{4,0},{8,4},{12,8},{16,12},{20,16},{24,20},{28,24},{32,28}... | collective-permute-start | bytes 6152 | tf_op jit(solution)/shard_map/ppermute | solution.py:33
  118.8 3.4 copy-start.3
  118.9 3.4 copy-start.9
  118.9 3.4 copy-start.11
  119.0 7.7 collective-permute-start.2
  123.3 7.7 collective-permute-start
  131.3 19.6 %collective-permute-start.5 = (f32[512,128]{0,1:T(8,128)S(1)}, f32[512,128]{0,1:T(8,128)S(1)}, u32[]{:S(2)}, u32[]{:S(2)}) collective-permute-start(f32[512,128]{0,1:T(8,128)S(1)} %convolution_add_fusion.14), channel_id=1, source_target_pairs={{0,764},{4,0},{8,4},{12,8},{16,12},{20,16},{24,20},{28,24},{32,28}... | collective-permute-start | bytes 786440 | tf_op jit(solution)/shard_map/ppermute | solution.py:33
  136.5 13.2 %collective-permute-start.7 = (bf16[2,512,128]{1,2,0:T(8,128)(2,1)S(1)}, bf16[2,512,128]{1,2,0:T(8,128)(2,1)S(1)}, u32[]{:S(2)}, u32[]{:S(2)}) collective-permute-start(bf16[2,512,128]{1,2,0:T(8,128)(2,1)S(1)} %collective-permute-done.2), channel_id=1, source_target_pairs={{4,0},{8,4},{12,8},{16,12},{20,16},{24,20},{28,24},{32,28},{36,32}... | collective-permute-start | bytes 786440 | tf_op jit(solution)/shard_map/ppermute | solution.py:28
  151.0 15.9 %collective-permute-start.10 = (f32[512,128]{0,1:T(8,128)S(1)}, f32[512,128]{0,1:T(8,128)S(1)}, u32[]{:S(2)}, u32[]{:S(2)}) collective-permute-start(f32[512,128]{0,1:T(8,128)S(1)} %add.105), channel_id=1, source_target_pairs={{0,764},{4,0},{8,4},{12,8},{16,12},{20,16},{24,20},{28,24},{32,28}... | collective-permute-start | bytes 786440 | tf_op jit(solution)/shard_map/ppermute | solution.py:33
  153.2 12.5 %collective-permute-start.12 = (bf16[2,512,128]{1,2,0:T(8,128)(2,1)S(1)}, bf16[2,512,128]{1,2,0:T(8,128)(2,1)S(1)}, u32[]{:S(2)}, u32[]{:S(2)}) collective-permute-start(bf16[2,512,128]{1,2,0:T(8,128)(2,1)S(1)} %collective-permute-done.7), channel_id=1, source_target_pairs={{4,0},{8,4},{12,8},{16,12},{20,16},{24,20},{28,24},{32,28},{36,32}... | collective-permute-start | bytes 786440 | tf_op jit(solution)/shard_map/ppermute | solution.py:28
  166.9 15.8 %collective-permute-start.15 = (f32[512,128]{0,1:T(8,128)S(1)}, f32[512,128]{0,1:T(8,128)S(1)}, u32[]{:S(2)}, u32[]{:S(2)}) collective-permute-start(f32[512,128]{0,1:T(8,128)S(1)} %add.107), channel_id=1, source_target_pairs={{0,764},{4,0},{8,4},{12,8},{16,12},{20,16},{24,20},{28,24},{32,28}... | collective-permute-start | bytes 786440 | tf_op jit(solution)/shard_map/ppermute | solution.py:33
  169.2 12.4 %collective-permute-start.17 = (bf16[2,512,128]{1,2,0:T(8,128)(2,1)S(1)}, bf16[2,512,128]{1,2,0:T(8,128)(2,1)S(1)}, u32[]{:S(2)}, u32[]{:S(2)}) collective-permute-start(bf16[2,512,128]{1,2,0:T(8,128)(2,1)S(1)} %collective-permute-done.12), channel_id=1, source_target_pairs={{4,0},{8,4},{12,8},{16,12},{20,16},{24,20},{28,24},{32,28},{36,32}... | collective-permute-start | bytes 786440 | tf_op jit(solution)/shard_map/ppermute | solution.py:28
  182.8 15.9 %collective-permute-start.20 = (f32[512,128]{0,1:T(8,128)S(1)}, f32[512,128]{0,1:T(8,128)S(1)}, u32[]{:S(2)}, u32[]{:S(2)}) collective-permute-start(f32[512,128]{0,1:T(8,128)S(1)} %add.109), channel_id=1, source_target_pairs={{0,764},{4,0},{8,4},{12,8},{16,12},{20,16},{24,20},{28,24},{32,28}... | collective-permute-start | bytes 786440 | tf_op jit(solution)/shard_map/ppermute | solution.py:33
  185.1 12.4 %collective-permute-start.22 = (bf16[2,512,128]{1,2,0:T(8,128)(2,1)S(1)}, bf16[2,512,128]{1,2,0:T(8,128)(2,1)S(1)}, u32[]{:S(2)}, u32[]{:S(2)}) collective-permute-start(bf16[2,512,128]{1,2,0:T(8,128)(2,1)S(1)} %collective-permute-done.17), channel_id=1, source_target_pairs={{4,0},{8,4},{12,8},{16,12},{20,16},{24,20},{28,24},{32,28},{36,32}... | collective-permute-start | bytes 786440 | tf_op jit(solution)/shard_map/ppermute | solution.py:28
  198.7 18.9 %collective-permute-start.25 = (f32[512,128]{0,1:T(8,128)S(1)}, f32[512,128]{0,1:T(8,128)S(1)}, u32[]{:S(2)}, u32[]{:S(2)}) collective-permute-start(f32[512,128]{0,1:T(8,128)S(1)} %add.111), channel_id=1, source_target_pairs={{0,764},{4,0},{8,4},{12,8},{16,12},{20,16},{24,20},{28,24},{32,28}... | collective-permute-start | bytes 786440 | tf_op jit(solution)/shard_map/ppermute | solution.py:33
  201.0 12.5 %collective-permute-start.27 = (bf16[2,512,128]{1,2,0:T(8,128)(2,1)S(1)}, bf16[2,512,128]{1,2,0:T(8,128)(2,1)S(1)}, u32[]{:S(2)}, u32[]{:S(2)}) collective-permute-start(bf16[2,512,128]{1,2,0:T(8,128)(2,1)S(1)} %collective-permute-done.22), channel_id=1, source_target_pairs={{4,0},{8,4},{12,8},{16,12},{20,16},{24,20},{28,24},{32,28},{36,32}... | collective-permute-start | bytes 786440 | tf_op jit(solution)/shard_map/ppermute | solution.py:28
  213.5 13.8 %copy-start.6 = (bf16[2,512,128]{1,2,0:T(8,128)(2,1)}, bf16[2,512,128]{1,2,0:T(8,128)(2,1)S(1)}, u32[]{:S(2)}) copy-start(bf16[2,512,128]{1,2,0:T(8,128)(2,1)S(1)} %collective-permute-done.27) | copy-start | bytes 786436
  213.8 8.5 %collective-permute-start.32 = (bf16[2,512,128]{1,2,0:T(8,128)(2,1)S(1)}, bf16[2,512,128]{1,2,0:T(8,128)(2,1)S(1)}, u32[]{:S(2)}, u32[]{:S(2)}) collective-permute-start(bf16[2,512,128]{1,2,0:T(8,128)(2,1)S(1)} %collective-permute-done.27), channel_id=1, source_target_pairs={{4,0},{8,4},{12,8},{16,12},{20,16},{24,20},{28,24},{32,28},{36,32}... | collective-permute-start | bytes 786440 | tf_op jit(solution)/shard_map/ppermute | solution.py:28
  217.7 7.7 collective-permute-start.30
  222.3 0.7 copy-start.7
  222.6 6.6 copy-start.4
  224.2 20.8 %copy-start.2 = (bf16[512,512]{1,0:T(8,128)(2,1)}, bf16[512,512]{1,0:T(8,128)(2,1)S(1)}, u32[]{:S(2)}) copy-start(bf16[512,512]{1,0:T(8,128)(2,1)S(1)} %fusion.22) | copy-start | bytes 1572868
  225.4 19.4 %collective-permute-start.35 = (f32[512,128]{0,1:T(8,128)S(1)}, f32[512,128]{0,1:T(8,128)S(1)}, u32[]{:S(2)}, u32[]{:S(2)}) collective-permute-start(f32[512,128]{0,1:T(8,128)S(1)} %add.115), channel_id=1, source_target_pairs={{0,28},{4,32},{8,36},{12,40},{16,44},{20,48},{24,52},{28,56},{32,6... | collective-permute-start | bytes 786440 | tf_op jit(solution)/shard_map/ppermute | solution.py:33
  246.5 3.5 copy-start.5
  246.5 3.5 copy-start.8
  246.5 3.5 copy-start.13
Sparse Core Ops, SparseCore 0:
  246.6 562.1 all-reduce.1
where the time goes:
time: 820 us; the launch traced here: 817 us
  waiting for transfers between devices  580 us (71%)
  starting transfers between devices  189 us (23%)
  matrix products  27.1 us (3%)
  between operations  15 us (2%)
    psum x1, waiting for transfers between devices, local(): weight_sum = lax.psum(weight_term, ('blk', 'fsdp'))  555 us
    ppermute x29, starting transfers between devices, from_behind(): lax.ppermute(value, axis, [(i, (i + by) % size) for i in range(size)])  118 us
    ppermute x7, starting transfers between devices, passed_along(): return lax.ppermute(value, axis, pairs)  62.3 us
    ppermute x29, waiting for transfers between devices, from_behind(): lax.ppermute(value, axis, [(i, (i + by) % size) for i in range(size)])  19.8 us
  transfers between devices with their start and end apart: 38, of which 11 were waited for; matrix products, arithmetic and copies ran while one was open for 3% of the time, Pallas kernels for 0%

commit v1 on v0

v1 whole, which is shorter than its diff:
```python
import jax
import jax.numpy as jnp
from jax import lax
from jax.experimental import pallas as pl
from jax.experimental.pallas import tpu as pltpu
from jax.sharding import PartitionSpec as P

ROUNDS = 8
LAG = 3
NX, NY, NZ, NF = 4, 8, 12, 4
PLANE = NX * NY * 2
MESH = pl.DeviceIdType.MESH
BF = jnp.bfloat16
F32 = jnp.float32
NT = (((1,), (1,)), ((), ()))
TILE = 128


def copy_to(src, dst, send, recv, blk, fsdp):
    return pltpu.make_async_remote_copy(
        src_ref=src, dst_ref=dst, send_sem=send, recv_sem=recv,
        device_id={"blk": blk, "fsdp": fsdp}, device_id_type=MESH)


def wide(column):
    return jnp.concatenate([column] * 4, axis=1)


def main_kernel(
    h_hbm, w_ref, gain_ref, k_ref, v_ref, do_ref, lse_ref, delta_ref, docs_ref,
    gp_ref, wfull, dk_ref, dv_ref, g3,
    h_ref, kb, vb, cb, ob, lb, eb, sb, qb,
    q_own, inv_s, normed_s, lse_c, delta_c, docs_c, dq_acc, dk_acc, dv_acc,
    own_half, csend, crecv, acc_s, xs, xr, a2_s, ys, yr, zs, zr, g1, g2,
    h_sem, f_send, f_recv, b_send, b_recv, fh_send, bh_send, q_send, q_recv, qh_send,
    w_send, w_recv, wc_send, wc_recv, c_sem, x_send, x_recv, y_send, y_recv, z_send, z_recv,
    gy_send, gy_recv, gx_send, gx_recv, gc_sem,
):
    p = lax.axis_index("blk")
    f = lax.axis_index("fsdp")
    last = lax.axis_size("blk") - 1
    c = lax.rem(p, 2)
    y = lax.rem(p // 2, NY)
    x = lax.rem(p // (2 * NY), NX)
    zh = p // PLANE
    z = zh * NF + f
    inpl = lax.rem(p, PLANE)
    scale = 128 ** -0.5

    def at_y(k):
        return p - 2 * y + 2 * lax.rem(y + k, NY)

    def at_x(k):
        return p - 2 * NY * x + 2 * NY * lax.rem(x + k, NX)

    def at_z(k):
        zz = lax.rem(z + k, NZ)
        return inpl + PLANE * (zz // NF), lax.rem(zz, NF)

    partner = p + 1 - 2 * c
    load_h = pltpu.make_async_copy(h_hbm, h_ref, h_sem)
    load_h.start()

    has_next = jnp.logical_and(p < last, inpl != PLANE - 1)
    has_prev = inpl != 0
    fwd_home = jnp.logical_and(inpl >= PLANE - 7, p + 7 <= last)
    bwd_home = jnp.logical_and(inpl < 7, p >= 7)
    fwd_gate = jnp.logical_and(inpl == 0, p > 0)
    bwd_gate = jnp.logical_and(inpl == PLANE - 1, p < last)
    fwd_to = (zh + 1) * PLANE
    bwd_to = zh * PLANE - 1

    barrier = pltpu.get_barrier_semaphore()

    def greet(blk, fsdp):
        pl.semaphore_signal(
            barrier, inc=1, device_id={"blk": blk, "fsdp": fsdp}, device_id_type=MESH)

    greet(partner, f)
    for k in range(1, NY):
        greet(at_y(k), f)
    for k in range(1, NX):
        greet(at_x(k), f)
    for k in range(1, NZ):
        greet(*at_z(k))
    pl.when(has_next)(lambda: greet(p + 1, f))
    pl.when(has_prev)(lambda: greet(p - 1, f))
    pl.when(fwd_home)(lambda: greet(fwd_to, f))
    pl.when(bwd_home)(lambda: greet(bwd_to, f))

    @pl.when(fwd_gate)
    def _():
        for k in range(1, 8):
            greet(p - k, f)

    @pl.when(bwd_gate)
    def _():
        for k in range(1, 8):
            greet(p + k, f)

    def count(flag, n):
        return jnp.where(flag, n, 0)

    pl.semaphore_wait(
        barrier,
        1 + (NY - 1) + (NX - 1) + (NZ - 1) + count(has_next, 1) + count(has_prev, 1)
        + count(fwd_home, 1) + count(bwd_home, 1) + count(fwd_gate, 7) + count(bwd_gate, 7))

    fwd_far = PLANE - inpl
    bwd_far = inpl + 1

    def fwd_step(d, srcs, to, slot, send):
        return [
            copy_to(src, buf.at[slot], send(i), f_recv.at[i, slot], to, f)
            for i, (src, buf) in enumerate(zip(srcs, (kb, vb, cb)))
        ]

    def bwd_step(d, srcs, to, slot, send):
        return [
            copy_to(src, buf.at[slot], send(i), b_recv.at[i, slot], to, f)
            for i, (src, buf) in enumerate(zip(srcs, (ob, lb, eb, sb)))
        ]

    own_fwd = (k_ref, v_ref, docs_ref)
    own_bwd = (do_ref, lse_ref, delta_ref, docs_ref)
    first_fwd = fwd_step(0, own_fwd, p + 1, 1, lambda i: f_send.at[i, 0])
    home_fwd = fwd_step(0, own_fwd, fwd_to, fwd_far, lambda i: fh_send.at[i])
    first_bwd = bwd_step(0, own_bwd, p - 1, 1, lambda i: b_send.at[i, 0])
    home_bwd = bwd_step(0, own_bwd, bwd_to, bwd_far, lambda i: bh_send.at[i])

    def start_all(copies):
        for one in copies:
            one.start()

    def finish_sends(copies):
        for one in copies:
            one.wait_send()

    pl.when(has_next)(lambda: start_all(first_fwd))
    pl.when(fwd_home)(lambda: start_all(home_fwd))
    pl.when(has_prev)(lambda: start_all(first_bwd))
    pl.when(bwd_home)(lambda: start_all(home_bwd))

    half = 256
    mine = pl.ds(pl.multiple_of(c * half, half), half)
    quarter = [pl.ds(pl.multiple_of(c * half + q * 128, 128), 128) for q in range(2)]
    w_copies = []
    for i, (k, rows) in enumerate(
        ((1, mine), (NZ - 1, mine), (2, quarter[0]), (NZ - 2, quarter[1]))
    ):
        w_copies.append(
            copy_to(w_ref.at[rows], wfull.at[f, rows], w_send.at[i], w_recv.at[i], *at_z(k)))
    start_all(w_copies)

    def as_columns(row):
        return jnp.broadcast_to(row, (128, row.shape[1])).T

    lse_c[...] = as_columns(lse_ref[...])
    delta_c[...] = as_columns(delta_ref[...])
    docs_c[...] = as_columns(docs_ref[...].astype(F32)).astype(jnp.int32)
    dk_acc[...] = jnp.zeros_like(dk_acc)
    dv_acc[...] = jnp.zeros_like(dv_acc)

    f1, f2, f3 = lax.rem(f + 1, NF), lax.rem(f + 2, NF), lax.rem(f + 3, NF)
    load_h.wait()
    wfull[f] = w_ref[...]

    def part(fs, w):
        cols = pl.ds(pl.multiple_of(fs * 512, 512), 512)
        return jnp.dot(h_ref[:, cols], w, preferred_element_type=F32)

    q_pre = part(f, w_ref[...])
    wc = [
        copy_to(wfull.at[fs, mine], wfull.at[fs, mine], wc_send.at[i], wc_recv.at[i], partner, f)
        for i, fs in enumerate((f3, f1, f2))
    ]
    w_copies[0].wait_recv()
    wc[0].start()
    w_copies[1].wait_recv()
    wc[1].start()
    w_copies[2].wait_recv()
    w_copies[3].wait_recv()
    wc[2].start()
    for i, fs in enumerate((f3, f1, f2)):
        wc[i].wait_recv()
        q_pre = q_pre + part(fs, wfull[fs])
    inv = lax.rsqrt(jnp.mean(q_pre * q_pre, axis=-1, keepdims=True) + 1e-06)
    normed = q_pre * inv
    q_own[...] = (normed * gain_ref[...]).astype(BF)
    normed_s[...] = normed
    inv_s[...] = jnp.broadcast_to(inv, inv_s.shape)

    def q_step(src, to, slot, send):
        return copy_to(src, qb.at[slot], send, q_recv.at[slot], to, f)

    first_q = q_step(q_own, p - 1, 1, q_send.at[0])
    home_q = q_step(q_own, bwd_to, bwd_far, qh_send)

    def dq_block(keys, values, docs_row, diagonal):
        for t in range(512 // TILE):
            rows = pl.ds(t * TILE, TILE)
            s = lax.dot_general(q_own[rows], keys[...], NT, preferred_element_type=F32) * scale
            allowed = wide(docs_c[rows]) == docs_row[...]
            if diagonal:
                i = lax.broadcasted_iota(jnp.int32, s.shape, 0) + t * TILE
                allowed = allowed & (i >= lax.broadcasted_iota(jnp.int32, s.shape, 1))
            prob = jnp.exp(jnp.where(allowed, s - wide(lse_c[rows]), -1e30))
            dp = lax.dot_general(do_ref[rows], values[...], NT, preferred_element_type=F32)
            ds = (prob * (dp - wide(delta_c[rows]))).astype(BF)
            term = jnp.dot(ds, keys[...], preferred_element_type=F32)
            if diagonal:
                dq_acc[rows] = term
            else:
                dq_acc[rows] += term

    dq_block(k_ref, v_ref, docs_ref, True)
    pl.when(has_prev)(lambda: first_q.start())
    pl.when(bwd_home)(lambda: home_q.start())

    def bwd_arrived(d):
        copies = bwd_step(d, (ob.at[d], lb.at[d], eb.at[d], sb.at[d]), p - 1, d + 1,
                          lambda i: b_send.at[i, d])
        return copies

    def take_q(d):
        @pl.when(p + d <= last)
        def _():
            q_step(q_own, p, d, q_send.at[0]).wait_recv()

        @pl.when(jnp.logical_and(jnp.logical_and(p + d <= last, has_prev), d < 7))
        def _():
            nxt = jnp.minimum(d + 1, 7)
            q_step(qb.at[d], p - 1, nxt, q_send.at[d]).start()

    def chain(d, carry):
        nxt = jnp.minimum(d + 1, 7)
        have_f = p >= d
        have_b = p + d <= last
        pass_f = jnp.logical_and(jnp.logical_and(have_f, has_next), d < 7)
        pass_b = jnp.logical_and(jnp.logical_and(have_b, has_prev), d < 7)
        fwd = fwd_step(d, (kb.at[d], vb.at[d], cb.at[d]), p + 1, nxt, lambda i: f_send.at[i, d])
        bwd = bwd_step(d, (ob.at[d], lb.at[d], eb.at[d], sb.at[d]), p - 1, nxt,
                       lambda i: b_send.at[i, d])
        f_in = fwd_step(d, own_fwd, p, d, lambda i: f_send.at[i, 0])
        b_in = bwd_step(d, own_bwd, p, d, lambda i: b_send.at[i, 0])
        for i in range(3):
            pl.when(have_f)(lambda: f_in[i].wait_recv())
            pl.when(pass_f)(lambda: fwd[i].start())
        for i in range(4):
            pl.when(have_b)(lambda: b_in[i].wait_recv())
            pl.when(pass_b)(lambda: bwd[i].start())
        pl.when(d > LAG)(lambda: take_q(d - LAG))
        pl.when(have_f)(lambda: dq_block(kb.at[d], vb.at[d], cb.at[d], False))
        return carry

    lax.fori_loop(1, 8, chain, 0)

    g = dq_acc[...] * scale * gain_ref[...]
    nrm = normed_s[...]
    grad_pre = inv_s[...] * (g - nrm * jnp.mean(g * nrm, axis=-1, keepdims=True))
    gp_ref[...] = grad_pre.astype(BF)
    gp_t = grad_pre.T.astype(BF)

    def product(side, fs):
        cols = pl.ds(pl.multiple_of(fs * 512 + side * 256, 256), 256)
        return jnp.dot(gp_t, h_ref[:, cols], preferred_element_type=F32)

    def dkv_block(q_ref, o_ref, lse_row, delta_row, docs_row, diagonal):
        for t in range(512 // TILE):
            rows = pl.ds(t * TILE, TILE)
            s = lax.dot_general(k_ref[rows], q_ref[...], NT, preferred_element_type=F32) * scale
            allowed = wide(docs_c[rows]) == docs_row[...]
            if diagonal:
                i = lax.broadcasted_iota(jnp.int32, s.shape, 0) + t * TILE
                allowed = allowed & (i <= lax.broadcasted_iota(jnp.int32, s.shape, 1))
            prob = jnp.exp(jnp.where(allowed, s - lse_row[...], -1e30))
            dp = lax.dot_general(v_ref[rows], o_ref[...], NT, preferred_element_type=F32)
            ds = (prob * (dp - delta_row[...])).astype(BF)
            dv_acc[rows] += jnp.dot(prob.astype(BF), o_ref[...], preferred_element_type=F32)
            dk_acc[rows] += jnp.dot(ds, q_ref[...], preferred_element_type=F32)

    def filler(lo, hi):
        def one(d, carry):
            pl.when(p + d <= last)(
                lambda: dkv_block(qb.at[d], ob.at[d], lb.at[d], eb.at[d], sb.at[d], False))
            return carry

        lax.fori_loop(lo, hi, one, 0)

    for fs in range(NF):
        csend[:, fs * 256:(fs + 1) * 256] = product(1 - c, fs).astype(BF)
    to_core = copy_to(csend, crecv, c_sem.at[0], c_sem.at[1], partner, f)
    to_core.start()
    take_q(5)
    for fs in range(NF):
        own_half[:, fs * 256:(fs + 1) * 256] = product(c, fs)
    dkv_block(q_own, do_ref, lse_ref, delta_ref, docs_ref, True)
    to_core.wait_recv()
    acc = own_half[...] + crecv[...].astype(F32)
    acc_s[...] = acc
    for xx in range(NX):
        xs[xx] = acc[32 * xx:32 * xx + 32].astype(BF)
    x_copies = [
        copy_to(xs.at[lax.rem(x + k, NX)], xr.at[k - 1], x_send.at[k - 1], x_recv.at[k - 1],
                at_x(k), f)
        for k in range(1, NX)
    ]
    start_all(x_copies)
    take_q(6)
    filler(1, 3)
    a2 = acc_s[pl.ds(pl.multiple_of(32 * x, 32), 32), :]
    for k in range(NX - 1):
        x_copies[k].wait_recv()
        a2 = a2 + xr[k].astype(F32)
    for yy in range(NY):
        for fs in range(NF):
            col = fs * 256 + 128 * (yy % 2)
            ys[yy, 8 * fs:8 * fs + 8] = a2[8 * (yy // 2):8 * (yy // 2) + 8, col:col + 128]
    y_copies = [
        copy_to(ys.at[lax.rem(y + k, NY)], yr.at[k - 1], y_send.at[k - 1], y_recv.at[k - 1],
                at_y(k), f)
        for k in range(1, NY)
    ]
    start_all(y_copies)
    take_q(7)
    filler(3, 5)
    a3 = ys[y]
    for k in range(NY - 1):
        y_copies[k].wait_recv()
        a3 = a3 + yr[k]
    zs[...] = a3
    z_copies = []
    for k in range(1, NZ):
        blk, fz = at_z(k)
        z_copies.append(
            copy_to(zs.at[pl.ds(pl.multiple_of(8 * fz, 8), 8)], zr.at[k - 1], z_send.at[k - 1],
                    z_recv.at[k - 1], blk, fz))
    start_all(z_copies)
    filler(5, 8)
    done = zs[pl.ds(pl.multiple_of(8 * f, 8), 8), :]
    for k in range(NZ - 1):
        z_copies[k].wait_recv()
        done = done + zr[k]
    g1[y] = done
    gy = [
        copy_to(g1.at[y], g1.at[y], gy_send.at[k - 1], gy_recv.at[k - 1], at_y(k), f)
        for k in range(1, NY)
    ]
    start_all(gy)
    dk_ref[...] = (dk_acc[...] * scale).astype(BF)
    dv_ref[...] = dv_acc[...].astype(BF)
    for one in gy:
        one.wait_recv()
    gx = [
        copy_to(g1, g2.at[x], gx_send.at[k - 1], gx_recv.at[k - 1], at_x(k), f)
        for k in range(1, NX)
    ]
    start_all(gx)
    g2[x] = g1[...]
    for one in gx:
        one.wait_recv()
    gc = copy_to(g2, g3.at[c], gc_sem.at[0], gc_sem.at[1], partner, f)
    gc.start()
    g3[c] = g2[...]

    pl.when(has_next)(lambda: finish_sends(first_fwd))
    pl.when(fwd_home)(lambda: finish_sends(home_fwd))
    pl.when(has_prev)(lambda: finish_sends(first_bwd))
    pl.when(bwd_home)(lambda: finish_sends(home_bwd))
    pl.when(has_prev)(lambda: first_q.wait_send())
    pl.when(bwd_home)(lambda: home_q.wait_send())
    finish_sends(w_copies)
    finish_sends(wc)

    def drained(d, carry):
        @pl.when(jnp.logical_and(p >= d, has_next))
        def _():
            finish_sends(fwd_step(d, (kb.at[d], vb.at[d], cb.at[d]), p + 1, d + 1,
                                  lambda i: f_send.at[i, d]))

        @pl.when(jnp.logical_and(p + d <= last, has_prev))
        def _():
            finish_sends(bwd_step(d, (ob.at[d], lb.at[d], eb.at[d], sb.at[d]), p - 1, d + 1,
                                  lambda i: b_send.at[i, d]))
            q_step(qb.at[d], p - 1, d + 1, q_send.at[d]).wait_send()

        return carry

    lax.fori_loop(1, 7, drained, 0)
    for group in ([to_core], x_copies, y_copies, z_copies, gy, gx, [gc]):
        finish_sends(group)
    gc.wait_recv()


def final_kernel(gp_ref, w_ref, dk_ref, dv_ref, g_ref, gh_out, dk_out, dv_out, wq_out):
    for fs in range(NF):
        gh_out[:, fs * 512:(fs + 1) * 512] = lax.dot_general(
            gp_ref[...], w_ref[fs], NT, preferred_element_type=F32).astype(BF)
    dk_out[...] = dk_ref[...]
    dv_out[...] = dv_ref[...]
    wq_out[...] = g_ref[...].reshape(128, 128).T


def local(
    hidden_in, w_query, query_gain, key_rows, value_rows, grad_out, logsumexp, row_delta, doc_ids
):
    vmem = pl.BlockSpec(memory_space=pltpu.VMEM)
    sds = jax.ShapeDtypeStruct
    dma = pltpu.SemaphoreType.DMA
    v = pltpu.VMEM
    tok = (512, 128)
    gp, wfull, dk, dv, g3 = pl.pallas_call(
        main_kernel,
        out_shape=[sds(tok, BF), sds((NF, 512, 128), BF), sds(tok, BF), sds(tok, BF),
                   sds((2, NX, NY, 8, 128), F32)],
        in_specs=[pl.BlockSpec(memory_space=pl.ANY)] + [vmem] * 8,
        out_specs=[vmem] * 5,
        scratch_shapes=[
            v((512, 2048), BF), v((8, *tok), BF), v((8, *tok), BF), v((8, 1, 512), jnp.int32),
            v((8, *tok), BF), v((8, 1, 512), F32), v((8, 1, 512), F32),
            v((8, 1, 512), jnp.int32), v((8, *tok), BF),
            v(tok, BF), v(tok, F32), v(tok, F32), v(tok, F32), v(tok, F32),
            v(tok, jnp.int32), v(tok, F32), v(tok, F32), v(tok, F32),
            v((128, 1024), F32), v((128, 1024), BF), v((128, 1024), BF), v((128, 1024), F32),
            v((NX, 32, 1024), BF), v((NX - 1, 32, 1024), BF), v((32, 1024), F32),
            v((NY, 32, 128), F32), v((NY - 1, 32, 128), F32),
            v((32, 128), F32), v((NZ - 1, 8, 128), F32),
            v((NY, 8, 128), F32), v((NX, NY, 8, 128), F32),
            dma, dma((3, 8)), dma((3, 8)), dma((4, 8)), dma((4, 8)), dma((3,)), dma((4,)),
            dma((8,)), dma((8,)), dma,
            dma((4,)), dma((4,)), dma((3,)), dma((3,)), dma((2,)),
            dma((NX - 1,)), dma((NX - 1,)), dma((NY - 1,)), dma((NY - 1,)),
            dma((NZ - 1,)), dma((NZ - 1,)), dma((NY - 1,)), dma((NY - 1,)),
            dma((NX - 1,)), dma((NX - 1,)), dma((2,)),
        ],
        compiler_params=pltpu.CompilerParams(
            collective_id=0, has_side_effects=True, vmem_limit_bytes=48 << 20),
        name="main",
    )(hidden_in[0], w_query, query_gain[None], key_rows[0], value_rows[0], grad_out[0],
      logsumexp, row_delta, doc_ids)

    row = pl.BlockSpec((128, 128), lambda i: (i, 0))
    whole = pl.BlockSpec((NF, 512, 128), lambda i: (0, 0, 0))
    gh, dk, dv, wq = pl.pallas_call(
        final_kernel,
        grid=(4,),
        out_shape=[sds((512, 2048), BF), sds(tok, BF), sds(tok, BF), sds(tok, F32)],
        in_specs=[row, whole, row, row,
                  pl.BlockSpec((1, NX, NY // 2, 1, 8, 128),
                               lambda i: (i // 2, 0, 0, i % 2, 0, 0))],
        out_specs=[pl.BlockSpec((128, 2048), lambda i: (i, 0)), row, row, row],
        name="finish",
    )(gp, wfull, dk, dv, g3.reshape(2, NX, NY // 2, 2, 8, 128))
    return gh[None], dk[None], dv[None], wq


def solution(mesh):
    return jax.shard_map(
        local,
        mesh=mesh,
        in_specs=(
            P("fsdp", "blk", None),
            P("fsdp", None),
            P(),
            P("fsdp", "blk", None),
            P("fsdp", "blk", None),
            P("fsdp", "blk", None),
            P("fsdp", "blk"),
            P("fsdp", "blk"),
            P("fsdp", "blk"),
        ),
        out_specs=(
            P("fsdp", "blk", None),
            P("fsdp", "blk", None),
            P("fsdp", "blk", None),
            P("fsdp", None),
        ),
        check_vma=False,
    )
```

time: 820 us -> 125 us (0.15)
  waiting for transfers between devices: 580 us -> 0 us
  starting transfers between devices: 189 us -> 0 us
  Pallas kernels: 0 us -> 112 us
  matrix products: 27.1 us -> 0 us
  between operations: 15 us -> 0.67 us
    psum x1 -> x0, waiting for transfers between devices: 555 us -> none  [local(): weight_sum = lax.psum(weight_term, ('blk', 'fsdp'))]
    ppermute x36 -> x0, starting transfers between devices: 181 us -> none  [the longest x29 118 us: from_behind(): lax.ppermute(value, axis, [(i, (i + by) % size) for i in range(size)])]
    pallas_call x0 -> x2, Pallas kernels: none -> 112 us  [the longest x1 108 us: local(): pl.pallas_call(main_kernel, out_shape=[sds(tok, BF), sds((NF, 512, 128),...]
    dot_general x43 -> x0, matrix products: 27.1 us -> none  [the longest x8 6.86 us: local(): lax.dot_general(prob_half, o_block, (((0,), (0,)), ((), ())), preferred_e...]
    ppermute x36 -> x0, waiting for transfers between devices: 24.8 us -> none  [the longest x29 19.8 us: from_behind(): lax.ppermute(value, axis, [(i, (i + by) % size) for i in range(size)])]
    unnamed x30 -> x28, local copies, waits for them, and re-layouts: 2.25 us -> 11.3 us
  transfers between devices with their start and end apart: 38 -> 0, of which waited for: 11 -> 0; matrix products, arithmetic and copies ran while one was open for 3% -> 0% of each run, Pallas kernels for 0% -> 0%
where the time goes in v1:
time: 125 us; the launch traced here: 124 us
  Pallas kernels  112 us (90%)
  local copies, waits for them, and re-layouts  11.3 us (9%)
    pallas_call x1, Pallas kernels, local(): pl.pallas_call(main_kernel, out_shape=[sds(tok, BF), sds((NF, 512, 128),...  108 us
    unnamed x28, local copies, waits for them, and re-layouts  11.3 us
    pallas_call x1, Pallas kernels, local(): pl.pallas_call(final_kernel, grid=(4,), out_shape=[sds((512, 2048), BF),...  4.32 us

profile of v1, /device:TPU:1, one launch (start us, length us, event | category | flops | bytes accessed | tf_op | source)
XLA Modules:
  0.0 124.2 jit_solution(14930695054194660442)
XLA Ops:
  0.6 0.0 copy-start
  0.6 1.6 %copy-done = bf16[1,512,2048]{2,1,0:T(8,128)(2,1)S(1)} copy-done((bf16[1,512,2048]{2,1,0:T(8,128)(2,1)S(1)}, bf16[1,512,2048]{2,1,0:T(8,128)(2,1)}, u32[]{:S(2)}) %copy-start) | copy-done | bytes 2097176
  2.2 0.0 copy-start.3
  2.2 0.9 copy-done.3
  3.1 0.0 copy-start.4
  3.1 0.9 copy-done.4
  4.0 0.0 copy-start.5
  4.0 0.9 copy-done.5
  4.9 0.0 copy-start.6
  4.9 0.9 copy-done.6
  5.8 0.0 copy-start.10
  5.8 0.7 copy-done.10
  6.5 0.0 copy-start.11
  6.5 0.7 copy-done.11
  7.2 0.0 copy-start.12
  7.2 0.7 copy-done.12
  7.9 0.0 copy-start.13
  7.9 0.7 copy-done.13
  8.5 107.9 %main.1 = (bf16[512,128]{1,0:T(8,128)(2,1)S(1)}, bf16[4,512,128]{2,1,0:T(8,128)(2,1)S(1)}, bf16[512,128]{1,0:T(8,128)(2,1)S(1)}, bf16[512,128]{1,0:T(8,128)(2,1)S(1)}, f32[2,4,8,8,128]{4,3,2,1,0:T(8,128)S(1)}) custom-call(bf16[512,2048]{1,0:T(8,128)(2,1)S(1)} %bitcast.9, bf16[512,128]{1,0:T(8,128)(2,1)S(1)} %copy-done.3, f32[1,128]{1,0:T(1,128)S(1)} %bitcast.14, ...), custom_call_target="tpu_custom_call" | custom-call | tf_op jit(solution)/shard_map/main/pallas_call | solution.py:412
  116.4 0.0 copy-start.1
  116.4 0.8 copy-done.1
  117.2 0.0 copy-start.2
  117.2 0.7 copy-done.2
  117.9 0.0 copy-start.7
  117.9 0.6 copy-done.7
  118.6 0.0 copy-start.8
  118.6 0.7 copy-done.8
  119.2 0.0 copy-start.9
  119.2 0.6 copy-done.9
  119.9 4.3 %finish.1 = (bf16[512,2048]{1,0:T(8,128)(2,1)}, bf16[512,128]{1,0:T(8,128)(2,1)}, bf16[512,128]{1,0:T(8,128)(2,1)}, f32[512,128]{1,0:T(8,128)}) custom-call(bf16[512,128]{1,0:T(8,128)(2,1)} %copy-done.7, bf16[4,512,128]{2,1,0:T(8,128)(2,1)} %copy-done.1, bf16[512,128]{1,0:T(8,128)(2,1)} %copy-done.8, bf16[512,128]{1,0:T(8,128)(2,1)} %copy-done.9, ...), custom_call_target="tpu_custom_call" | custom-call | tf_op jit(solution)/shard_map/finish/pallas_call | solution.py:444
Async XLA Ops:
  0.6 1.6 %copy-start = (bf16[1,512,2048]{2,1,0:T(8,128)(2,1)S(1)}, bf16[1,512,2048]{2,1,0:T(8,128)(2,1)}, u32[]{:S(2)}) copy-start(bf16[1,512,2048]{2,1,0:T(8,128)(2,1)} %param.9) | copy-start | bytes 6291460
  2.2 0.9 copy-start.3
  3.1 0.9 copy-start.4
  4.0 0.9 copy-start.5
  4.9 0.9 copy-start.6
  5.8 0.7 copy-start.10
  6.5 0.7 copy-start.11
  7.2 0.7 copy-start.12
  7.9 0.7 copy-start.13
  116.4 0.8 copy-start.1
  117.2 0.7 copy-start.2
  117.9 0.6 copy-start.7
  118.6 0.7 copy-start.8
  119.2 0.6 copy-start.9

commit v2 on v1

--- a/solution.py
+++ b/solution.py
@@ -9,11 +9,15 @@
 LAG = 3
 NX, NY, NZ, NF = 4, 8, 12, 4
 PLANE = NX * NY * 2
+GIVER = {1: 63, 2: 46, 3: 61, 4: 28, 5: 11, 6: 42, 7: 57}
+HOME = {d: PLANE - d for d in GIVER}
+DIRECT = [d for d in GIVER if GIVER[d] == HOME[d]]
+VIA = [d for d in GIVER if GIVER[d] != HOME[d]]
 MESH = pl.DeviceIdType.MESH
 BF = jnp.bfloat16
 F32 = jnp.float32
 NT = (((1,), (1,)), ((), ()))
-TILE = 128
+TILE = 512
 
 
 def copy_to(src, dst, send, recv, blk, fsdp):
@@ -27,12 +31,15 @@
 
 
 def main_kernel(
-    h_hbm, w_ref, gain_ref, k_ref, v_ref, do_ref, lse_ref, delta_ref, docs_ref,
-    gp_ref, wfull, dk_ref, dv_ref, g3,
-    h_ref, kb, vb, cb, ob, lb, eb, sb, qb,
+    h_hbm, w_hbm, gain_hbm, k_hbm, v_hbm, do_hbm, lse_hbm, delta_hbm, docs_hbm,
+    gh_ref, dk_ref, dv_ref, g3,
+    h_ref, w_ref, gain_ref, k_ref, v_ref, do_ref, lse_ref, delta_ref, docs_ref,
+    wfull, gp_ref, kb, vb, cb, ob, lb, eb, sb, qb,
     q_own, inv_s, normed_s, lse_c, delta_c, docs_c, dq_acc, dk_acc, dv_acc,
-    own_half, csend, crecv, acc_s, xs, xr, a2_s, ys, yr, zs, zr, g1, g2,
-    h_sem, f_send, f_recv, b_send, b_recv, fh_send, bh_send, q_send, q_recv, qh_send,
+    own_half, csend, crecv, acc_s, xs, xr, y_own, ys, yr, zs, zr, g1, g2,
+    hk, hv, hc, ho, hl, he, hs, hq,
+    l_sem, f_send, f_recv, b_send, b_recv, fh_send, bh_send, q_send, q_recv, qh_send,
+    hf_send, hf_recv, hb_send, hb_recv,
     w_send, w_recv, wc_send, wc_recv, c_sem, x_send, x_recv, y_send, y_recv, z_send, z_recv,
     gy_send, gy_recv, gx_send, gx_recv, gc_sem,
 ):
@@ -58,13 +65,46 @@
         return inpl + PLANE * (zz // NF), lax.rem(zz, NF)
 
     partner = p + 1 - 2 * c
-    load_h = pltpu.make_async_copy(h_hbm, h_ref, h_sem)
-    load_h.start()
+    loads = [
+        pltpu.make_async_copy(src, dst, l_sem.at[i])
+        for i, (src, dst) in enumerate((
+            (w_hbm, w_ref), (h_hbm, h_ref), (k_hbm, k_ref), (v_hbm, v_ref), (do_hbm, do_ref),
+            (lse_hbm, lse_ref), (delta_hbm, delta_ref), (docs_hbm, docs_ref),
+            (gain_hbm, gain_ref)))
+    ]
+    for one in loads:
+        one.start()
 
     has_next = jnp.logical_and(p < last, inpl != PLANE - 1)
     has_prev = inpl != 0
-    fwd_home = jnp.logical_and(inpl >= PLANE - 7, p + 7 <= last)
-    bwd_home = jnp.logical_and(inpl < 7, p >= 7)
+    up, down = zh < NZ // NF - 1, zh > 0
+    mirror = PLANE - 1 - inpl
+
+    def among(values, at):
+        hit = at == values[0]
+        for one in values[1:]:
+            hit = jnp.logical_or(hit, at == one)
+        return hit
+
+    def lookup(pairs, at):
+        out = jnp.int32(0)
+        for key, value in pairs:
+            out = out + jnp.where(at == key, value, 0)
+        return out
+
+    def roles(on, at):
+        direct = jnp.logical_and(on, among([HOME[d] for d in DIRECT], at))
+        via = jnp.logical_and(on, among([HOME[d] for d in VIA], at))
+        middle = jnp.logical_and(on, among([GIVER[d] for d in VIA], at))
+        to_middle = lookup([(HOME[d], GIVER[d] - HOME[d]) for d in VIA], at)
+        to_home = lookup([(GIVER[d], HOME[d] - GIVER[d]) for d in VIA], at)
+        slot = lookup([(GIVER[d], d) for d in VIA], at)
+        return direct, via, middle, to_middle, to_home, slot
+
+    fwd_direct, fwd_via, fwd_mid, off, back, fwd_slot = roles(up, inpl)
+    fwd_mid_at, fwd_home_at = p + off, p + back
+    bwd_direct, bwd_via, bwd_mid, off, back, bwd_slot = roles(down, mirror)
+    bwd_mid_at, bwd_home_at = p - off, p - back
     fwd_gate = jnp.logical_and(inpl == 0, p > 0)
     bwd_gate = jnp.logical_and(inpl == PLANE - 1, p < last)
     fwd_to = (zh + 1) * PLANE
@@ -85,26 +125,30 @@
         greet(*at_z(k))
     pl.when(has_next)(lambda: greet(p + 1, f))
     pl.when(has_prev)(lambda: greet(p - 1, f))
-    pl.when(fwd_home)(lambda: greet(fwd_to, f))
-    pl.when(bwd_home)(lambda: greet(bwd_to, f))
+    pl.when(jnp.logical_or(fwd_direct, fwd_mid))(lambda: greet(fwd_to, f))
+    pl.when(jnp.logical_or(bwd_direct, bwd_mid))(lambda: greet(bwd_to, f))
+    pl.when(fwd_via)(lambda: greet(fwd_mid_at, f))
+    pl.when(fwd_mid)(lambda: greet(fwd_home_at, f))
+    pl.when(bwd_via)(lambda: greet(bwd_mid_at, f))
+    pl.when(bwd_mid)(lambda: greet(bwd_home_at, f))
 
     @pl.when(fwd_gate)
     def _():
-        for k in range(1, 8):
-            greet(p - k, f)
+        for d in GIVER:
+            greet(p - PLANE + GIVER[d], f)
 
     @pl.when(bwd_gate)
     def _():
-        for k in range(1, 8):
-            greet(p + k, f)
-
-    def count(flag, n):
-        return jnp.where(flag, n, 0)
-
-    pl.semaphore_wait(
-        barrier,
-        1 + (NY - 1) + (NX - 1) + (NZ - 1) + count(has_next, 1) + count(has_prev, 1)
-        + count(fwd_home, 1) + count(bwd_home, 1) + count(fwd_gate, 7) + count(bwd_gate, 7))
+        for d in GIVER:
+            greet(p + PLANE - GIVER[d], f)
+
+    peers = 1 + (NY - 1) + (NX - 1) + (NZ - 1)
+    for flag, n in (
+        (has_next, 1), (has_prev, 1), (fwd_direct, 1), (bwd_direct, 1), (fwd_mid, 2),
+        (bwd_mid, 2), (fwd_via, 1), (bwd_via, 1), (fwd_gate, 7), (bwd_gate, 7),
+    ):
+        peers = peers + jnp.where(flag, n, 0)
+    pl.semaphore_wait(barrier, peers)
 
     fwd_far = PLANE - inpl
     bwd_far = inpl + 1
@@ -121,12 +165,22 @@
             for i, (src, buf) in enumerate(zip(srcs, (ob, lb, eb, sb)))
         ]
 
-    own_fwd = (k_ref, v_ref, docs_ref)
-    own_bwd = (do_ref, lse_ref, delta_ref, docs_ref)
+    own_fwd = (k_hbm, v_hbm, docs_hbm)
+    own_bwd = (do_hbm, lse_hbm, delta_hbm, docs_hbm)
     first_fwd = fwd_step(0, own_fwd, p + 1, 1, lambda i: f_send.at[i, 0])
     home_fwd = fwd_step(0, own_fwd, fwd_to, fwd_far, lambda i: fh_send.at[i])
+    via_fwd = [
+        copy_to(src, buf, fh_send.at[i], hf_recv.at[i], fwd_mid_at, f)
+        for i, (src, buf) in enumerate(zip(own_fwd, (hk, hv, hc)))
+    ]
+    mid_fwd = fwd_step(0, (hk, hv, hc), fwd_to, fwd_slot, lambda i: hf_send.at[i])
     first_bwd = bwd_step(0, own_bwd, p - 1, 1, lambda i: b_send.at[i, 0])
     home_bwd = bwd_step(0, own_bwd, bwd_to, bwd_far, lambda i: bh_send.at[i])
+    via_bwd = [
+        copy_to(src, buf, bh_send.at[i], hb_recv.at[i], bwd_mid_at, f)
+        for i, (src, buf) in enumerate(zip(own_bwd, (ho, hl, he, hs)))
+    ]
+    mid_bwd = bwd_step(0, (ho, hl, he, hs), bwd_to, bwd_slot, lambda i: hb_send.at[i])
 
     def start_all(copies):
         for one in copies:
@@ -136,10 +190,42 @@
         for one in copies:
             one.wait_send()
 
+    def hand_on(arriving, leaving):
+        for i in range(len(leaving)):
+            arriving[i].wait_recv()
+            leaving[i].start()
+
+    pl.when(fwd_direct)(lambda: start_all(home_fwd))
+    pl.when(fwd_via)(lambda: start_all(via_fwd))
     pl.when(has_next)(lambda: start_all(first_fwd))
-    pl.when(fwd_home)(lambda: start_all(home_fwd))
+    pl.when(bwd_direct)(lambda: start_all(home_bwd))
+    pl.when(bwd_via)(lambda: start_all(via_bwd))
     pl.when(has_prev)(lambda: start_all(first_bwd))
-    pl.when(bwd_home)(lambda: start_all(home_bwd))
+
+    def take_fwd(d):
+        nxt = jnp.minimum(d + 1, 7)
+        have = p >= d
+        onward = jnp.logical_and(jnp.logical_and(have, has_next), d < 7)
+        leave = fwd_step(d, (kb.at[d], vb.at[d], cb.at[d]), p + 1, nxt, lambda i: f_send.at[i, d])
+        arrive = fwd_step(d, own_fwd, p, d, lambda i: f_send.at[i, 0])
+        for i in range(3):
+            pl.when(have)(lambda: arrive[i].wait_recv())
+            pl.when(onward)(lambda: leave[i].start())
+
+    def theirs(d, crossing):
+        far = inpl + d > PLANE - 1
+        return jnp.logical_and(p + d <= last, far if crossing else jnp.logical_not(far))
+
+    def take_bwd(d, crossing):
+        nxt = jnp.minimum(d + 1, 7)
+        have = theirs(d, crossing)
+        onward = jnp.logical_and(jnp.logical_and(have, has_prev), d < 7)
+        leave = bwd_step(d, (ob.at[d], lb.at[d], eb.at[d], sb.at[d]), p - 1, nxt,
+                         lambda i: b_send.at[i, d])
+        arrive = bwd_step(d, own_bwd, p, d, lambda i: b_send.at[i, 0])
+        for i in range(4):
+            pl.when(have)(lambda: arrive[i].wait_recv())
+            pl.when(onward)(lambda: leave[i].start())
 
     half = 256
     mine = pl.ds(pl.multiple_of(c * half, half), half)
@@ -149,8 +235,11 @@
         ((1, mine), (NZ - 1, mine), (2, quarter[0]), (NZ - 2, quarter[1]))
     ):
         w_copies.append(
-            copy_to(w_ref.at[rows], wfull.at[f, rows], w_send.at[i], w_recv.at[i], *at_z(k)))
+            copy_to(w_hbm.at[rows], wfull.at[f, rows], w_send.at[i], w_recv.at[i], *at_z(k)))
     start_all(w_copies)
+
+    for one in loads:
+        one.wait()
 
     def as_columns(row):
         return jnp.broadcast_to(row, (128, row.shape[1])).T
@@ -161,8 +250,12 @@
     dk_acc[...] = jnp.zeros_like(dk_acc)
     dv_acc[...] = jnp.zeros_like(dv_acc)
 
+    take_fwd(1)
+    pl.when(fwd_mid)(lambda: hand_on(via_fwd, mid_fwd))
+    take_bwd(1, False)
+    pl.when(bwd_mid)(lambda: hand_on(via_bwd, mid_bwd))
+
     f1, f2, f3 = lax.rem(f + 1, NF), lax.rem(f + 2, NF), lax.rem(f + 3, NF)
-    load_h.wait()
     wfull[f] = w_ref[...]
 
     def part(fs, w):
@@ -181,6 +274,8 @@
     w_copies[2].wait_recv()
     w_copies[3].wait_recv()
     wc[2].start()
+    take_fwd(2)
+    take_bwd(2, False)
     for i, fs in enumerate((f3, f1, f2)):
         wc[i].wait_recv()
         q_pre = q_pre + part(fs, wfull[fs])
@@ -195,6 +290,8 @@
 
     first_q = q_step(q_own, p - 1, 1, q_send.at[0])
     home_q = q_step(q_own, bwd_to, bwd_far, qh_send)
+    via_q = copy_to(q_own, hq, qh_send, hb_recv.at[4], bwd_mid_at, f)
+    mid_q = q_step(hq, bwd_to, bwd_slot, hb_send.at[4])
 
     def dq_block(keys, values, docs_row, diagonal):
         for t in range(512 // TILE):
@@ -215,45 +312,37 @@
 
     dq_block(k_ref, v_ref, docs_ref, True)
     pl.when(has_prev)(lambda: first_q.start())
-    pl.when(bwd_home)(lambda: home_q.start())
-
-    def bwd_arrived(d):
-        copies = bwd_step(d, (ob.at[d], lb.at[d], eb.at[d], sb.at[d]), p - 1, d + 1,
-                          lambda i: b_send.at[i, d])
-        return copies
-
-    def take_q(d):
-        @pl.when(p + d <= last)
+    pl.when(bwd_direct)(lambda: home_q.start())
+    pl.when(bwd_via)(lambda: via_q.start())
+
+    def take_q(d, crossing):
+        have = theirs(d, crossing)
+
+        @pl.when(have)
         def _():
             q_step(q_own, p, d, q_send.at[0]).wait_recv()
 
-        @pl.when(jnp.logical_and(jnp.logical_and(p + d <= last, has_prev), d < 7))
+        @pl.when(jnp.logical_and(jnp.logical_and(have, has_prev), d < 7))
         def _():
             nxt = jnp.minimum(d + 1, 7)
             q_step(qb.at[d], p - 1, nxt, q_send.at[d]).start()
 
+    def dq_far(d, carry):
+        pl.when(p >= d)(lambda: dq_block(kb.at[d], vb.at[d], cb.at[d], False))
+        return carry
+
+    take_fwd(3)
+    take_bwd(3, False)
+    lax.fori_loop(1, 4, dq_far, 0)
+
     def chain(d, carry):
-        nxt = jnp.minimum(d + 1, 7)
-        have_f = p >= d
-        have_b = p + d <= last
-        pass_f = jnp.logical_and(jnp.logical_and(have_f, has_next), d < 7)
-        pass_b = jnp.logical_and(jnp.logical_and(have_b, has_prev), d < 7)
-        fwd = fwd_step(d, (kb.at[d], vb.at[d], cb.at[d]), p + 1, nxt, lambda i: f_send.at[i, d])
-        bwd = bwd_step(d, (ob.at[d], lb.at[d], eb.at[d], sb.at[d]), p - 1, nxt,
-                       lambda i: b_send.at[i, d])
-        f_in = fwd_step(d, own_fwd, p, d, lambda i: f_send.at[i, 0])
-        b_in = bwd_step(d, own_bwd, p, d, lambda i: b_send.at[i, 0])
-        for i in range(3):
-            pl.when(have_f)(lambda: f_in[i].wait_recv())
-            pl.when(pass_f)(lambda: fwd[i].start())
-        for i in range(4):
-            pl.when(have_b)(lambda: b_in[i].wait_recv())
-            pl.when(pass_b)(lambda: bwd[i].start())
-        pl.when(d > LAG)(lambda: take_q(d - LAG))
-        pl.when(have_f)(lambda: dq_block(kb.at[d], vb.at[d], cb.at[d], False))
-        return carry
-
-    lax.fori_loop(1, 8, chain, 0)
+        take_fwd(d)
+        take_bwd(d, False)
+        take_q(d - LAG, False)
+        pl.when(jnp.logical_and(d == 5, bwd_mid))(lambda: hand_on([via_q], [mid_q]))
+        return dq_far(d, carry)
+
+    lax.fori_loop(4, 8, chain, 0)
 
     g = dq_acc[...] * scale * gain_ref[...]
     nrm = normed_s[...]
@@ -279,10 +368,18 @@
             dv_acc[rows] += jnp.dot(prob.astype(BF), o_ref[...], preferred_element_type=F32)
             dk_acc[rows] += jnp.dot(ds, q_ref[...], preferred_element_type=F32)
 
-    def filler(lo, hi):
+    def filler(lo, hi, crossing):
         def one(d, carry):
-            pl.when(p + d <= last)(
+            pl.when(theirs(d, crossing))(
                 lambda: dkv_block(qb.at[d], ob.at[d], lb.at[d], eb.at[d], sb.at[d], False))
+            return carry
+
+        lax.fori_loop(lo, hi, one, 0)
+
+    def cross(lo, hi):
+        def one(d, carry):
+            take_bwd(d, True)
+            take_q(d, True)
             return carry
 
         lax.fori_loop(lo, hi, one, 0)
@@ -291,10 +388,9 @@
         csend[:, fs * 256:(fs + 1) * 256] = product(1 - c, fs).astype(BF)
     to_core = copy_to(csend, crecv, c_sem.at[0], c_sem.at[1], partner, f)
     to_core.start()
-    take_q(5)
+    take_q(5, False)
     for fs in range(NF):
         own_half[:, fs * 256:(fs + 1) * 256] = product(c, fs)
-    dkv_block(q_own, do_ref, lse_ref, delta_ref, docs_ref, True)
     to_core.wait_recv()
     acc = own_half[...] + crecv[...].astype(F32)
     acc_s[...] = acc
@@ -306,8 +402,8 @@
         for k in range(1, NX)
     ]
     start_all(x_copies)
-    take_q(6)
-    filler(1, 3)
+    take_q(6, False)
+    dkv_block(q_own, do_ref, lse_ref, delta_ref, docs_ref, True)
     a2 = acc_s[pl.ds(pl.multiple_of(32 * x, 32), 32), :]
     for k in range(NX - 1):
         x_copies[k].wait_recv()
@@ -315,19 +411,20 @@
     for yy in range(NY):
         for fs in range(NF):
             col = fs * 256 + 128 * (yy % 2)
-            ys[yy, 8 * fs:8 * fs + 8] = a2[8 * (yy // 2):8 * (yy // 2) + 8, col:col + 128]
+            y_own[yy, 8 * fs:8 * fs + 8] = a2[8 * (yy // 2):8 * (yy // 2) + 8, col:col + 128]
+        ys[yy] = y_own[yy].astype(BF)
     y_copies = [
         copy_to(ys.at[lax.rem(y + k, NY)], yr.at[k - 1], y_send.at[k - 1], y_recv.at[k - 1],
                 at_y(k), f)
         for k in range(1, NY)
     ]
     start_all(y_copies)
-    take_q(7)
-    filler(3, 5)
-    a3 = ys[y]
+    take_q(7, False)
+    filler(1, 4, False)
+    a3 = y_own[y]
     for k in range(NY - 1):
         y_copies[k].wait_recv()
-        a3 = a3 + yr[k]
+        a3 = a3 + yr[k].astype(F32)
     zs[...] = a3
     z_copies = []
     for k in range(1, NZ):
@@ -336,17 +433,24 @@
             copy_to(zs.at[pl.ds(pl.multiple_of(8 * fz, 8), 8)], zr.at[k - 1], z_send.at[k - 1],
                     z_recv.at[k - 1], blk, fz))
     start_all(z_copies)
-    filler(5, 8)
+    cross(1, 5)
+    filler(4, 8, False)
+    filler(1, 5, True)
     done = zs[pl.ds(pl.multiple_of(8 * f, 8), 8), :]
     for k in range(NZ - 1):
         z_copies[k].wait_recv()
         done = done + zr[k]
-    g1[y] = done
+    g1[y // 2, lax.rem(y, 2)] = done
     gy = [
-        copy_to(g1.at[y], g1.at[y], gy_send.at[k - 1], gy_recv.at[k - 1], at_y(k), f)
+        copy_to(g1.at[y // 2, lax.rem(y, 2)], g1.at[y // 2, lax.rem(y, 2)], gy_send.at[k - 1], gy_recv.at[k - 1], at_y(k), f)
         for k in range(1, NY)
     ]
     start_all(gy)
+    cross(5, 8)
+    filler(5, 8, True)
+    for fs in range(NF):
+        gh_ref[:, fs * 512:(fs + 1) * 512] = lax.dot_general(
+            gp_ref[...], wfull[fs], NT, preferred_element_type=F32).astype(BF)
     dk_ref[...] = (dk_acc[...] * scale).astype(BF)
     dv_ref[...] = dv_acc[...].astype(BF)
     for one in gy:
@@ -364,11 +468,14 @@
     g3[c] = g2[...]
 
     pl.when(has_next)(lambda: finish_sends(first_fwd))
-    pl.when(fwd_home)(lambda: finish_sends(home_fwd))
+    pl.when(fwd_direct)(lambda: finish_sends(home_fwd))
+    pl.when(fwd_via)(lambda: finish_sends(via_fwd))
+    pl.when(fwd_mid)(lambda: finish_sends(mid_fwd))
     pl.when(has_prev)(lambda: finish_sends(first_bwd))
-    pl.when(bwd_home)(lambda: finish_sends(home_bwd))
+    pl.when(bwd_direct)(lambda: finish_sends(home_bwd + [home_q]))
+    pl.when(bwd_via)(lambda: finish_sends(via_bwd + [via_q]))
+    pl.when(bwd_mid)(lambda: finish_sends(mid_bwd + [mid_q]))
     pl.when(has_prev)(lambda: first_q.wait_send())
-    pl.when(bwd_home)(lambda: home_q.wait_send())
     finish_sends(w_copies)
     finish_sends(wc)
 
@@ -392,65 +499,75 @@
     gc.wait_recv()
 
 
-def final_kernel(gp_ref, w_ref, dk_ref, dv_ref, g_ref, gh_out, dk_out, dv_out, wq_out):
-    for fs in range(NF):
-        gh_out[:, fs * 512:(fs + 1) * 512] = lax.dot_general(
-            gp_ref[...], w_ref[fs], NT, preferred_element_type=F32).astype(BF)
-    dk_out[...] = dk_ref[...]
-    dv_out[...] = dv_ref[...]
-    wq_out[...] = g_ref[...].reshape(128, 128).T
+def final_kernel(gh_ref, dk_ref, dv_ref, g_ref, gh_out, dk_out, dv_out, wq_out, wq, sem):
+    puts = [
+        pltpu.make_async_copy(src, dst, sem.at[i])
+        for i, (src, dst) in enumerate(
+            ((gh_ref, gh_out), (dk_ref, dk_out), (dv_ref, dv_out), (wq, wq_out)))
+    ]
+    for one in puts[:3]:
+        one.start()
+    for i in range(4):
+        block = g_ref[i // 2, :, :, i % 2].reshape(128, 128)
+        wq[i * 128:(i + 1) * 128, :] = block.T
+    puts[3].start()
+    for one in puts:
+        one.wait()
 
 
 def local(
     hidden_in, w_query, query_gain, key_rows, value_rows, grad_out, logsumexp, row_delta, doc_ids
 ):
     vmem = pl.BlockSpec(memory_space=pltpu.VMEM)
+    hbm = pl.BlockSpec(memory_space=pltpu.HBM)
     sds = jax.ShapeDtypeStruct
     dma = pltpu.SemaphoreType.DMA
     v = pltpu.VMEM
     tok = (512, 128)
-    gp, wfull, dk, dv, g3 = pl.pallas_call(
+    gh, dk, dv, g3 = pl.pallas_call(
         main_kernel,
-        out_shape=[sds(tok, BF), sds((NF, 512, 128), BF), sds(tok, BF), sds(tok, BF),
-                   sds((2, NX, NY, 8, 128), F32)],
-        in_specs=[pl.BlockSpec(memory_space=pl.ANY)] + [vmem] * 8,
-        out_specs=[vmem] * 5,
+        out_shape=[sds((512, 2048), BF), sds(tok, BF), sds(tok, BF),
+                   sds((2, NX, NY // 2, 2, 8, 128), F32)],
+        in_specs=[hbm] * 9,
+        out_specs=[vmem] * 4,
         scratch_shapes=[
-            v((512, 2048), BF), v((8, *tok), BF), v((8, *tok), BF), v((8, 1, 512), jnp.int32),
+            v((512, 2048), BF), v(tok, BF), v((1, 128), F32), v(tok, BF), v(tok, BF), v(tok, BF),
+            v((1, 512), F32), v((1, 512), F32), v((1, 512), jnp.int32),
+            v((NF, 512, 128), BF), v(tok, BF), v((8, *tok), BF), v((8, *tok), BF), v((8, 1, 512), jnp.int32),
             v((8, *tok), BF), v((8, 1, 512), F32), v((8, 1, 512), F32),
             v((8, 1, 512), jnp.int32), v((8, *tok), BF),
             v(tok, BF), v(tok, F32), v(tok, F32), v(tok, F32), v(tok, F32),
             v(tok, jnp.int32), v(tok, F32), v(tok, F32), v(tok, F32),
             v((128, 1024), F32), v((128, 1024), BF), v((128, 1024), BF), v((128, 1024), F32),
-            v((NX, 32, 1024), BF), v((NX - 1, 32, 1024), BF), v((32, 1024), F32),
-            v((NY, 32, 128), F32), v((NY - 1, 32, 128), F32),
+            v((NX, 32, 1024), BF), v((NX - 1, 32, 1024), BF), v((NY, 32, 128), F32),
+            v((NY, 32, 128), BF), v((NY - 1, 32, 128), BF),
             v((32, 128), F32), v((NZ - 1, 8, 128), F32),
-            v((NY, 8, 128), F32), v((NX, NY, 8, 128), F32),
-            dma, dma((3, 8)), dma((3, 8)), dma((4, 8)), dma((4, 8)), dma((3,)), dma((4,)),
-            dma((8,)), dma((8,)), dma,
+            v((NY // 2, 2, 8, 128), F32), v((NX, NY // 2, 2, 8, 128), F32),
+            v(tok, BF), v(tok, BF), v((1, 512), jnp.int32), v(tok, BF), v((1, 512), F32),
+            v((1, 512), F32), v((1, 512), jnp.int32), v(tok, BF),
+            dma((9,)), dma((3, 8)), dma((3, 8)), dma((4, 8)), dma((4, 8)), dma((3,)), dma((4,)),
+            dma((8,)), dma((8,)), dma, dma((3,)), dma((3,)), dma((5,)), dma((5,)),
             dma((4,)), dma((4,)), dma((3,)), dma((3,)), dma((2,)),
             dma((NX - 1,)), dma((NX - 1,)), dma((NY - 1,)), dma((NY - 1,)),
             dma((NZ - 1,)), dma((NZ - 1,)), dma((NY - 1,)), dma((NY - 1,)),
             dma((NX - 1,)), dma((NX - 1,)), dma((2,)),
         ],
         compiler_params=pltpu.CompilerParams(
-            collective_id=0, has_side_effects=True, vmem_limit_bytes=48 << 20),
+            collective_id=0, has_side_effects=True, vmem_limit_bytes=40 << 20),
         name="main",
-    )(hidden_in[0], w_query, query_gain[None], key_rows[0], value_rows[0], grad_out[0],
-      logsumexp, row_delta, doc_ids)
-
-    row = pl.BlockSpec((128, 128), lambda i: (i, 0))
-    whole = pl.BlockSpec((NF, 512, 128), lambda i: (0, 0, 0))
+    )(*(pltpu.with_memory_space_constraint(a, pltpu.HBM) for a in (
+        hidden_in[0], w_query, query_gain[None], key_rows[0], value_rows[0], grad_out[0],
+        logsumexp, row_delta, doc_ids)))
+
     gh, dk, dv, wq = pl.pallas_call(
         final_kernel,
-        grid=(4,),
         out_shape=[sds((512, 2048), BF), sds(tok, BF), sds(tok, BF), sds(tok, F32)],
-        in_specs=[row, whole, row, row,
-                  pl.BlockSpec((1, NX, NY // 2, 1, 8, 128),
-                               lambda i: (i // 2, 0, 0, i % 2, 0, 0))],
-        out_specs=[pl.BlockSpec((128, 2048), lambda i: (i, 0)), row, row, row],
+        in_specs=[vmem] * 4,
+        out_specs=[hbm] * 4,
+        scratch_shapes=[v(tok, F32), dma((4,))],
+        compiler_params=pltpu.CompilerParams(vmem_limit_bytes=4 << 20),
         name="finish",
-    )(gp, wfull, dk, dv, g3.reshape(2, NX, NY // 2, 2, 8, 128))
+    )(gh, dk, dv, g3)
     return gh[None], dk[None], dv[None], wq
 
 

time: 125 us -> 96.3 us (0.77)
  Pallas kernels: 112 us -> 95.5 us
  local copies, waits for them, and re-layouts: 11.3 us -> 0 us
    pallas_call x2, Pallas kernels: 112 us -> 95.5 us  [the longest x1 94 us: local(): pl.pallas_call(main_kernel, out_shape=[sds((512, 2048), BF), sds(tok, BF)...]
    unnamed x28 -> x0, local copies, waits for them, and re-layouts: 11.3 us -> none
where the time goes in v2:
time: 96.3 us; the launch traced here: 96.2 us
  Pallas kernels  95.5 us (99%)
    pallas_call x1, Pallas kernels, local(): pl.pallas_call(main_kernel, out_shape=[sds((512, 2048), BF), sds(tok, BF)...  94 us

profile of v2, /device:TPU:1, one launch (start us, length us, event | category | flops | bytes accessed | tf_op | source)
XLA Modules:
  0.0 96.2 jit_solution(13649406171036633076)
XLA Ops:
  0.6 94.0 %main.1 = (bf16[512,2048]{1,0:T(8,128)(2,1)S(1)}, bf16[512,128]{1,0:T(8,128)(2,1)S(1)}, bf16[512,128]{1,0:T(8,128)(2,1)S(1)}, f32[2,4,4,2,8,128]{5,4,3,2,1,0:T(8,128)S(1)}) custom-call(bf16[512,2048]{1,0:T(8,128)(2,1)} %bitcast.8, bf16[512,128]{1,0:T(8,128)(2,1)} %w_hbm.1, f32[1,128]{1,0:T(1,128)} %bitcast.12, bf16[512,128]{1,0:T(8,128)(2,1)} %bitcast.9, ...), custom_call_target="tpu_custom_call" | custom-call | tf_op jit(solution)/shard_map/main/pallas_call | solution.py:527
  94.6 1.5 %finish.1 = (bf16[512,2048]{1,0:T(8,128)(2,1)}, bf16[512,128]{1,0:T(8,128)(2,1)}, bf16[512,128]{1,0:T(8,128)(2,1)}, f32[512,128]{1,0:T(8,128)}) custom-call(bf16[512,2048]{1,0:T(8,128)(2,1)S(1)} %get-tuple-element.12.gh_ref, bf16[512,128]{1,0:T(8,128)(2,1)S(1)} %get-tuple-element.13.dk_ref, bf16[512,128]{1,0:T(8,128)(2,1)S(1)} %get-tuple-element.14.dv_ref, ...), custom_call_target="tpu_custom_call" | custom-call | tf_op jit(solution)/shard_map/finish/pallas_call | solution.py:562

commit v3 on v2

--- a/solution.py
+++ b/solution.py
@@ -6,7 +6,6 @@
 from jax.sharding import PartitionSpec as P
 
 ROUNDS = 8
-LAG = 3
 NX, NY, NZ, NF = 4, 8, 12, 4
 PLANE = NX * NY * 2
 GIVER = {1: 63, 2: 46, 3: 61, 4: 28, 5: 11, 6: 42, 7: 57}
@@ -252,7 +251,6 @@
 
     take_fwd(1)
     pl.when(fwd_mid)(lambda: hand_on(via_fwd, mid_fwd))
-    take_bwd(1, False)
     pl.when(bwd_mid)(lambda: hand_on(via_bwd, mid_bwd))
 
     f1, f2, f3 = lax.rem(f + 1, NF), lax.rem(f + 2, NF), lax.rem(f + 3, NF)
@@ -275,7 +273,6 @@
     w_copies[3].wait_recv()
     wc[2].start()
     take_fwd(2)
-    take_bwd(2, False)
     for i, fs in enumerate((f3, f1, f2)):
         wc[i].wait_recv()
         q_pre = q_pre + part(fs, wfull[fs])
@@ -327,18 +324,20 @@
             nxt = jnp.minimum(d + 1, 7)
             q_step(qb.at[d], p - 1, nxt, q_send.at[d]).start()
 
+    def take_rows(d):
+        take_bwd(d, False)
+        take_q(d, False)
+
     def dq_far(d, carry):
         pl.when(p >= d)(lambda: dq_block(kb.at[d], vb.at[d], cb.at[d], False))
         return carry
 
     take_fwd(3)
-    take_bwd(3, False)
     lax.fori_loop(1, 4, dq_far, 0)
 
     def chain(d, carry):
         take_fwd(d)
-        take_bwd(d, False)
-        take_q(d - LAG, False)
+        pl.when(lax.rem(d, 2) == 0)(lambda: take_rows(d // 2 - 1))
         pl.when(jnp.logical_and(d == 5, bwd_mid))(lambda: hand_on([via_q], [mid_q]))
         return dq_far(d, carry)
 
@@ -376,19 +375,31 @@
 
         lax.fori_loop(lo, hi, one, 0)
 
-    def cross(lo, hi):
-        def one(d, carry):
-            take_bwd(d, True)
-            take_q(d, True)
+    before = PLANE - 1 - inpl
+    turn = (before + 1) // 2
+
+    def cross(k):
+        def take(d, carry):
+            @pl.when(turn == k)
+            def _():
+                take_bwd(d, True)
+                take_q(d, True)
+
             return carry
 
-        lax.fori_loop(lo, hi, one, 0)
+        def use(d, carry):
+            pl.when(jnp.logical_and(turn == k, theirs(d, True)))(
+                lambda: dkv_block(qb.at[d], ob.at[d], lb.at[d], eb.at[d], sb.at[d], False))
+            return carry
+
+        lax.fori_loop(1, 8, take, 0)
+        lax.fori_loop(1, 8, use, 0)
 
     for fs in range(NF):
         csend[:, fs * 256:(fs + 1) * 256] = product(1 - c, fs).astype(BF)
     to_core = copy_to(csend, crecv, c_sem.at[0], c_sem.at[1], partner, f)
     to_core.start()
-    take_q(5, False)
+    take_rows(3)
     for fs in range(NF):
         own_half[:, fs * 256:(fs + 1) * 256] = product(c, fs)
     to_core.wait_recv()
@@ -402,7 +413,7 @@
         for k in range(1, NX)
     ]
     start_all(x_copies)
-    take_q(6, False)
+    take_rows(4)
     dkv_block(q_own, do_ref, lse_ref, delta_ref, docs_ref, True)
     a2 = acc_s[pl.ds(pl.multiple_of(32 * x, 32), 32), :]
     for k in range(NX - 1):
@@ -419,8 +430,9 @@
         for k in range(1, NY)
     ]
     start_all(y_copies)
-    take_q(7, False)
+    take_rows(5)
     filler(1, 4, False)
+    cross(0)
     a3 = y_own[y]
     for k in range(NY - 1):
         y_copies[k].wait_recv()
@@ -433,9 +445,11 @@
             copy_to(zs.at[pl.ds(pl.multiple_of(8 * fz, 8), 8)], zr.at[k - 1], z_send.at[k - 1],
                     z_recv.at[k - 1], blk, fz))
     start_all(z_copies)
-    cross(1, 5)
-    filler(4, 8, False)
-    filler(1, 5, True)
+    take_rows(6)
+    filler(4, 6, False)
+    take_rows(7)
+    filler(6, 8, False)
+    cross(1)
     done = zs[pl.ds(pl.multiple_of(8 * f, 8), 8), :]
     for k in range(NZ - 1):
         z_copies[k].wait_recv()
@@ -446,13 +460,10 @@
         for k in range(1, NY)
     ]
     start_all(gy)
-    cross(5, 8)
-    filler(5, 8, True)
+    cross(2)
     for fs in range(NF):
         gh_ref[:, fs * 512:(fs + 1) * 512] = lax.dot_general(
             gp_ref[...], wfull[fs], NT, preferred_element_type=F32).astype(BF)
-    dk_ref[...] = (dk_acc[...] * scale).astype(BF)
-    dv_ref[...] = dv_acc[...].astype(BF)
     for one in gy:
         one.wait_recv()
     gx = [
@@ -461,6 +472,9 @@
     ]
     start_all(gx)
     g2[x] = g1[...]
+    cross(3)
+    dk_ref[...] = (dk_acc[...] * scale).astype(BF)
+    dv_ref[...] = dv_acc[...].astype(BF)
     for one in gx:
         one.wait_recv()
     gc = copy_to(g2, g3.at[c], gc_sem.at[0], gc_sem.at[1], partner, f)

time: 96.3 us -> 95.5 us (level)
  the two profiles are of different devices: /device:TPU:1 before, /device:TPU:41 now
where the time goes in v3:
time: 95.5 us; the launch traced here: 95.4 us
  Pallas kernels  94.8 us (99%)
    pallas_call x1, Pallas kernels, local(): pl.pallas_call(main_kernel, out_shape=[sds((512, 2048), BF), sds(tok, BF)...  93.3 us

profile of v3, /device:TPU:41, one launch (start us, length us, event | category | flops | bytes accessed | tf_op | source)
XLA Modules:
  0.0 95.4 jit_solution(17604905959991829988)
XLA Ops:
  0.6 93.3 %main.1 = (bf16[512,2048]{1,0:T(8,128)(2,1)S(1)}, bf16[512,128]{1,0:T(8,128)(2,1)S(1)}, bf16[512,128]{1,0:T(8,128)(2,1)S(1)}, f32[2,4,4,2,8,128]{5,4,3,2,1,0:T(8,128)S(1)}) custom-call(bf16[512,2048]{1,0:T(8,128)(2,1)} %bitcast.8, bf16[512,128]{1,0:T(8,128)(2,1)} %w_hbm.1, f32[1,128]{1,0:T(1,128)} %bitcast.12, bf16[512,128]{1,0:T(8,128)(2,1)} %bitcast.9, ...), custom_call_target="tpu_custom_call" | custom-call | tf_op jit(solution)/shard_map/main/pallas_call | solution.py:541
  93.9 1.5 %finish.1 = (bf16[512,2048]{1,0:T(8,128)(2,1)}, bf16[512,128]{1,0:T(8,128)(2,1)}, bf16[512,128]{1,0:T(8,128)(2,1)}, f32[512,128]{1,0:T(8,128)}) custom-call(bf16[512,2048]{1,0:T(8,128)(2,1)S(1)} %get-tuple-element.12.gh_ref, bf16[512,128]{1,0:T(8,128)(2,1)S(1)} %get-tuple-element.13.dk_ref, bf16[512,128]{1,0:T(8,128)(2,1)S(1)} %get-tuple-element.14.dv_ref, ...), custom_call_target="tpu_custom_call" | custom-call | tf_op jit(solution)/shard_map/finish/pallas_call | solution.py:576
